TPU v7x, 32 devices: a whole 2x2x4 slice. The times are simulated.
32 devices in a mesh: row: 16 (over z, y, x), col: 2 (over core).
Axes of the slice: x: 2, y: 2, z: 4, core: 2. Of those that a mesh axis runs over, the one named last changes fastest.
Arguments:
- vectors_in: bfloat16 [32768, 2048], P('row', 'col'), may hold values from -6 to 6
- panel: bfloat16 [32768, 256], P('row', 'col'), may hold values from -0.03125 to 0.03125
- factor: float32 [256, 256], replicated, may hold values from -3 to 8, as said below
- atom_basis: int32 [16, 128], P('row'), may hold values from 1 to 24, 2048 in all within a row
- proj_count: int32 [2048], P('row'), may hold values from 1 to 16
- coupling: bfloat16 [2048, 9, 384], P('row'), may hold values from -0.4375 to 0.4375
- block_present: int32 [2048, 9], P('row'), may hold values 0 or 1
- occ_mask: int32 [2048], P('col'), may hold values 0 or 1
- occ_weight: float32 [2048], P('col'), may hold values from 0.5 to 2
Outputs:
- vectors: bfloat16 [32768, 2048], P('row', 'col')
- density: float32 [2048, 256], P(('row', 'col'))
Inputs may be any that keep to these rules, and one draw needn't show every extreme that they name: `factor`: zero below the diagonal; the diagonal lies in 4 to 8. `atom_basis`: each row sums to 2048, and 24 is reached in each row.
All inputs are finite; a program needn't handle non-finite values. No bound on the sum of `block_present` or of `occ_mask` on one device may be relied on, other than what follows from the above.
Results may differ from a plain program's by a relative error of at most 0.0075.
Values may be sent and summed in bfloat16 or wider, within the bound.
A program may use at most 192 MiB of HBM per device.

v0:
```python
import jax
import jax.numpy as jnp
from jax import lax
from jax.sharding import PartitionSpec as P

NPMAX = 16
BMAX = 24
K = 9


def with_halo(array, sides, width):
    for axis, dim in sides:
        devices, length = (lax.axis_size(axis), array.shape[dim])
        up = [(i, (i + 1) % devices) for i in range(devices)]
        down = [(j, i) for i, j in up]
        last = lax.slice_in_dim(array, length - width, length, axis=dim)
        first = lax.slice_in_dim(array, 0, width, axis=dim)
        before = lax.ppermute(last, axis, up)
        after = lax.ppermute(first, axis, down)
        array = jnp.concatenate([before, array, after], axis=dim)
    return array


def panel_product(fragment, columns):
    return lax.dot_general(
        fragment, columns, (((0,), (0,)), ((), ())), preferred_element_type=jnp.float32
    )


def local(
    vectors_in, panel, factor, atom_basis, proj_count, coupling, block_present, occ_mask, occ_weight
):
    rows_here = vectors_in.shape[0]
    cols_here = vectors_in.shape[1]
    whole_panel = lax.all_gather(panel, "col", axis=1, tiled=True)
    inner_products = panel_product(whole_panel, vectors_in)
    inner_products = lax.psum(inner_products, "row")
    mixing = jnp.dot(factor.T, inner_products, precision=lax.Precision.HIGHEST).astype(jnp.bfloat16)
    update = jnp.dot(whole_panel, mixing, preferred_element_type=jnp.float32)
    vectors = (vectors_in.astype(jnp.float32) - update).astype(jnp.bfloat16)
    counts = atom_basis[0]
    atoms_here = counts.shape[0]
    starts = jnp.cumsum(counts) - counts
    slot_rank = jnp.arange(BMAX, dtype=jnp.int32)
    row_index = jnp.where(
        slot_rank[None, :] < counts[:, None], starts[:, None] + slot_rank[None, :], rows_here
    )
    padded = jnp.take(vectors, row_index.reshape(-1), axis=0, mode="fill", fill_value=0).reshape(
        atoms_here, BMAX, cols_here
    )
    rim_width = (K - 1) // 2
    extended = with_halo(padded, (("row", 0),), rim_width)
    projections = jnp.zeros((atoms_here, NPMAX, cols_here), jnp.float32)
    for relative in range(K):
        blocks = coupling[:, relative].reshape(atoms_here, NPMAX, BMAX)
        blocks = jnp.where(
            block_present[:, relative, None, None] > 0, blocks, jnp.zeros_like(blocks)
        )
        neighbours = extended[relative : relative + atoms_here]
        projections = projections + jnp.einsum(
            "aij,ajn->ain", blocks, neighbours, preferred_element_type=jnp.float32
        )
    kept_rows = (jnp.arange(NPMAX, dtype=jnp.int32)[None, :] < proj_count[:, None]).astype(
        jnp.float32
    )
    rounded = (projections * kept_rows[:, :, None]).astype(jnp.bfloat16)
    column_total = cols_here * lax.axis_size("col")
    weights = occ_mask.astype(jnp.float32) * occ_weight / column_total
    weighted = (rounded * weights[None, None, :]).astype(jnp.bfloat16)
    partial_value = jnp.einsum(
        "ain,ajn->aij", weighted, rounded, preferred_element_type=jnp.float32
    )
    partial_value = partial_value.reshape(atoms_here, NPMAX * NPMAX)
    density = lax.psum_scatter(
        partial_value.astype(jnp.bfloat16), "col", scatter_dimension=0, tiled=True
    ).astype(jnp.float32)
    return (vectors, density)


def solution(mesh):
    placed = (
        P("row", "col"),
        P("row", "col"),
        P(),
        P("row", None),
        P("row"),
        P("row", None, None),
        P("row", None),
        P("col"),
        P("col"),
    )
    return jax.shard_map(
        local,
        mesh=mesh,
        in_specs=placed,
        out_specs=(P("row", "col"), P(("row", "col"), None)),
        check_vma=False,
    )
```

profile of v0, /device:TPU:0, one launch (start us, length us, event | category | flops | bytes accessed | tf_op | source)
XLA Modules:
  0.0 292.0 jit_solution(12120854242485173018)
XLA Ops:
  10.6 1.4 fusion.48
  13.7 6.5 %copy.39 = bf16[2048,1024]{0,1:T(8,128)(2,1)} copy(bf16[2048,1024]{1,0:T(8,128)(2,1)} %param.9) | data formatting | bytes 8388608 | tf_op args[0]
  21.7 1.2 copy.45
  23.6 1.2 copy.53
  28.7 4.8 %fusion.51 = f32[256,1024]{1,0:T(8,128)} fusion(bf16[2048,256]{1,0:T(8,128)(2,1)} %all-gather.2.cloned.1.call-done, bf16[2048,1024]{1,0:T(8,128)(2,1)} %param.9), kind=kOutput, calls=%fused_computation.88 | convolution fusion | flops 1073741824 | bytes 6291456 | tf_op jit(solution)/shard_map/dot_general | solution.py:25
  33.8 115.1 %all-reduce.2.cloned.1.call-done = f32[256,1024]{1,0:T(8,128)} async-done(((f32[256,1024]{1,0:T(8,128)}), f32[256,1024]{1,0:T(8,128)}) %all-reduce.2.cloned.1.call-update) | async-done | bytes 1048592 | tf_op jit(solution)/shard_map/psum | solution.py:37
  148.9 3.0 %convolution_convert_fusion = bf16[1024,256]{1,0:T(8,128)(2,1)S(1)} fusion(f32[256,1024]{1,0:T(8,128)} %all-reduce.2.cloned.1.call-done, f32[256,256]{1,0:T(8,128)S(1)} %copy-done), kind=kOutput, calls=%fused_computation.45 | convolution fusion | flops 805568512 | bytes 1835008 | tf_op jit(solution)/shard_map/dot_general | solution.py:38
  152.0 5.4 %fusion = bf16[2048,1024]{0,1:T(8,128)(2,1)} fusion(bf16[2048,1024]{0,1:T(8,128)(2,1)} %copy.39, bf16[1024,256]{1,0:T(8,128)(2,1)S(1)} %convolution_convert_fusion, bf16[2048,256]{1,0:T(8,128)(2,1)S(1)} %copy-done.4), kind=kOutput, calls=%fused_computation.8 | convolution fusion | flops 1080033280 | bytes 9961472 | tf_op jit(solution)/shard_map/dot_general | solution.py:39
  157.4 6.4 %copy.61 = bf16[2048,1024]{1,0:T(8,128)(2,1)} copy(bf16[2048,1024]{0,1:T(8,128)(2,1)} %fusion) | data formatting | bytes 8388608
  163.8 18.7 %gather_fusion = bf16[3072,1024]{1,0:T(8,128)(2,1)} fusion(bf16[2048,1024]{1,0:T(8,128)(2,1)} %copy.61, s32[3072]{0:T(1024)S(1)} %broadcast_clamp_fusion), kind=kCustom, calls=%fused_computation | custom fusion | bytes 12595200 | tf_op jit(solution)/shard_map/jit(_take)/gather | solution.py:48
  182.4 4.1 %broadcast_select_fusion = bf16[3072,1024]{1,0:T(8,128)(2,1)S(1)} fusion(bf16[3072,1024]{1,0:T(8,128)(2,1)} %gather_fusion, pred[3072]{0:T(1024)(128)(4,1)S(1)} %compare_and_fusion.1), kind=kLoop, calls=%fused_computation.36 | loop fusion | flops 3145728 | bytes 12585984 | tf_op jit(solution)/shard_map/jit(_take)/select_n | solution.py:48
  186.5 1.5 collective-permute-start
  188.1 4.1 %collective-permute-start.1 = (bf16[4,24,1024]{2,1,0:T(8,128)(2,1)S(1)}, bf16[4,24,1024]{2,1,0:T(8,128)(2,1)S(1)}, u32[]{:S(2)}, u32[]{:S(2)}) collective-permute-start(bf16[4,24,1024]{2,1,0:T(8,128)(2,1)S(1)} %bitcast.69), channel_id=1, source_target_pairs={{2,0},{4,2},{6,4},{8,6},{10,8},{12,10},{14,12},{16,14},{18,16},{20... | collective-permute-start | bytes 589832 | tf_op jit(solution)/shard_map/ppermute | solution.py:19
  193.0 2.9 collective-permute-done
  195.9 4.3 %fusion.12 = f32[128,16,1024]{2,1,0:T(8,128)} fusion(bf16[128,16,24]{2,1,0:T(8,128)(2,1)S(1)} %copy.47, bf16[4,24,1024]{2,1,0:T(8,128)(2,1)S(1)} %collective-permute-done, bf16[128,24,1024]{2,1,0:T(8,128)(2,1)S(1)} %broadcast_select_fusion.1), kind=kOutput, calls=%fused_computation.19 | convolution fusion | flops 103809024 | bytes 14974976 | tf_op jit(solution)/shard_map/aij,ajn->ain/dot_general | solution.py:60
  200.2 4.3 %fusion.15 = f32[128,16,1024]{2,1,0:T(8,128)} fusion(bf16[128,16,24]{2,1,0:T(8,128)(2,1)S(1)} %copy-done.5, bf16[4,24,1024]{2,1,0:T(8,128)(2,1)S(1)} %collective-permute-done, bf16[128,24,1024]{2,1,0:T(8,128)(2,1)S(1)} %broadcast_select_fusion.1), kind=kOutput, calls=%fused_computation.21 | convolution fusion | flops 103809024 | bytes 14974976 | tf_op jit(solution)/shard_map/aij,ajn->ain/dot_general | solution.py:60
  204.4 4.3 %fusion.18 = f32[128,16,1024]{2,1,0:T(8,128)} fusion(bf16[128,16,24]{2,1,0:T(8,128)(2,1)S(1)} %copy-done.6, bf16[4,24,1024]{2,1,0:T(8,128)(2,1)S(1)} %collective-permute-done, bf16[128,24,1024]{2,1,0:T(8,128)(2,1)S(1)} %broadcast_select_fusion.1), kind=kOutput, calls=%fused_computation.23 | convolution fusion | flops 103809024 | bytes 14974976 | tf_op jit(solution)/shard_map/aij,ajn->ain/dot_general | solution.py:60
  208.8 4.3 %fusion.25 = f32[128,16,1024]{2,1,0:T(8,128)} fusion(bf16[128,16,24]{2,1,0:T(8,128)(2,1)S(1)} %copy.49, bf16[128,24,1024]{2,1,0:T(8,128)(2,1)S(1)} %broadcast_select_fusion.1, bf16[4,24,1024]{2,1,0:T(8,128)(2,1)S(1)} %collective-permute-done), kind=kOutput, calls=%fused_computation.31 | convolution fusion | flops 103809024 | bytes 14974976 | tf_op jit(solution)/shard_map/aij,ajn->ain/dot_general | solution.py:60
  213.1 4.3 %fusion.6 = f32[128,16,1024]{2,1,0:T(8,128)} fusion(bf16[128,16,24]{2,1,0:T(8,128)(2,1)S(1)} %copy-done.7, bf16[4,24,1024]{2,1,0:T(8,128)(2,1)S(1)} %collective-permute-done.1, bf16[128,24,1024]{2,1,0:T(8,128)(2,1)S(1)} %broadcast_select_fusion.1), kind=kOutput, calls=%fused_computation.15 | convolution fusion | flops 103809024 | bytes 14974976 | tf_op jit(solution)/shard_map/aij,ajn->ain/dot_general | solution.py:60
  217.4 4.3 %fusion.9 = f32[128,16,1024]{2,1,0:T(8,128)} fusion(bf16[128,16,24]{2,1,0:T(8,128)(2,1)S(1)} %copy-done.8, bf16[4,24,1024]{2,1,0:T(8,128)(2,1)S(1)} %collective-permute-done.1, bf16[128,24,1024]{2,1,0:T(8,128)(2,1)S(1)} %broadcast_select_fusion.1), kind=kOutput, calls=%fused_computation.17 | convolution fusion | flops 103809024 | bytes 14974976 | tf_op jit(solution)/shard_map/aij,ajn->ain/dot_general | solution.py:60
  221.6 4.3 %fusion.3 = f32[128,16,1024]{2,1,0:T(8,128)} fusion(bf16[128,16,24]{2,1,0:T(8,128)(2,1)S(1)} %copy-done.9, bf16[4,24,1024]{2,1,0:T(8,128)(2,1)S(1)} %collective-permute-done.1, bf16[128,24,1024]{2,1,0:T(8,128)(2,1)S(1)} %broadcast_select_fusion.1), kind=kOutput, calls=%fused_computation.13 | convolution fusion | flops 103809024 | bytes 14974976 | tf_op jit(solution)/shard_map/aij,ajn->ain/dot_general | solution.py:60
  225.9 4.3 %fusion.20 = f32[128,16,1024]{2,1,0:T(8,128)} fusion(bf16[128,16,24]{2,1,0:T(8,128)(2,1)S(1)} %copy.59, bf16[4,24,1024]{2,1,0:T(8,128)(2,1)S(1)} %collective-permute-done.1, bf16[128,24,1024]{2,1,0:T(8,128)(2,1)S(1)} %broadcast_select_fusion.1), kind=kOutput, calls=%fused_computation.25 | convolution fusion | flops 103809024 | bytes 14974976 | tf_op jit(solution)/shard_map/aij,ajn->ain/dot_general | solution.py:60
  230.2 46.4 %fusion.37 = bf16[128,16,16]{2,1,0:T(8,128)(2,1)S(1)} fusion(f32[128,16,1024]{2,1,0:T(8,128)} %fusion.20, f32[128,16,1024]{2,1,0:T(8,128)} %fusion.3, f32[128,16,1024]{2,1,0:T(8,128)} %fusion.9, f32[128,16,1024]{2,1,0:T(8,128)} %fusion.6, f32[128,16,1024]{2,1,0:T(8,128)} %fusion.25, f32[128,16,1024]{2,1,0:T(8,128)} %fusion.12, ...), kind=kOutput, calls=%fused_computation.46 | convolution fusion | flops 316702720 | bytes 73576448 | tf_op jit(solution)/shard_map/ain,ajn->aij/dot_general | solution.py:70
  277.8 6.1 %reduce-scatter.4.cloned.1.call-done = bf16[64,256]{1,0:T(8,128)(2,1)} async-done(((bf16[128,256]{1,0:T(8,128)(2,1)}), bf16[64,256]{1,0:T(8,128)(2,1)}) %reduce-scatter.4.cloned.1.call-update) | async-done | bytes 32784
  (77 shorter events, 14.8 us)
Async XLA Ops:
  7.2 141.7 %copy-start = (f32[256,256]{1,0:T(8,128)S(1)}, f32[256,256]{1,0:T(8,128)}, u32[]{:S(2)}) copy-start(f32[256,256]{1,0:T(8,128)} %param.11) | copy-start | bytes 786436
  7.2 21.5 %all-gather.2.cloned.1.call-start = ((), (), s32[]{:S(2)}) async-start(), calls=%async_computation.1 | async-start | bytes 1572864 | tf_op jit(solution)/shard_map/all_gather | solution.py:35
  7.9 141.0 %all-reduce.2.cloned.1.call-start = ((), (), s32[]{:S(2)}) async-start(), calls=%async_computation.2 | async-start | bytes 2097152 | tf_op jit(solution)/shard_map/psum | solution.py:37
  13.7 14.8 %copy-start.11 = (f32[1024]{0:T(1024)S(1)}, f32[1024]{0:T(1024)}, u32[]{:S(2)}) copy-start(f32[1024]{0:T(1024)} %param.17) | copy-start | bytes 12292
  13.7 14.8 %copy-start.12 = (s32[1024]{0:T(1024)S(1)}, s32[1024]{0:T(1024)}, u32[]{:S(2)}) copy-start(s32[1024]{0:T(1024)} %param.16) | copy-start | bytes 12292
  13.7 14.8 %copy-start.10 = (s32[1,128]{1,0:T(1,128)S(1)}, s32[1,128]{1,0:T(1,128)}, u32[]{:S(2)}) copy-start(s32[1,128]{1,0:T(1,128)} %param.12) | copy-start | bytes 1540
  24.8 8.8 %copy-start.13 = (s32[128]{0:T(128)S(1)}, s32[128]{0:T(128)}, u32[]{:S(2)}) copy-start(s32[128]{0:T(128)} %param.13) | copy-start | bytes 1540
  28.7 123.2 %copy-start.4 = (bf16[2048,256]{1,0:T(8,128)(2,1)S(1)}, bf16[2048,256]{1,0:T(8,128)(2,1)}, u32[]{:S(2)}) copy-start(bf16[2048,256]{1,0:T(8,128)(2,1)} %all-gather.2.cloned.1.call-done) | copy-start | bytes 3145732
  33.6 250.3 %reduce-scatter.4.cloned.1.call-start = ((), (), s32[]{:S(2)}) async-start(), calls=%async_computation.3 | async-start | bytes 98304
  182.4 9.8 %copy-start.3 = (bf16[3072,1024]{1,0:T(8,128)(2,1)S(1)}, bf16[3072,1024]{1,0:T(8,128)(2,1)}, u32[]{:S(2)}) copy-start(bf16[3072,1024]{1,0:T(8,128)(2,1)} %gather_fusion) | copy-start | bytes 18874372
  186.5 9.3 %collective-permute-start = (bf16[4,24,1024]{2,1,0:T(8,128)(2,1)S(1)}, bf16[4,24,1024]{2,1,0:T(8,128)(2,1)S(1)}, u32[]{:S(2)}, u32[]{:S(2)}) collective-permute-start(bf16[4,24,1024]{2,1,0:T(8,128)(2,1)S(1)} %bitcast.70), channel_id=1, source_target_pairs={{0,2},{2,4},{4,6},{6,8},{8,10},{10,12},{12,14},{14,16},{16,18},{18... | collective-permute-start | bytes 589832 | tf_op jit(solution)/shard_map/ppermute | solution.py:18
  188.1 25.0 %collective-permute-start.1 = (bf16[4,24,1024]{2,1,0:T(8,128)(2,1)S(1)}, bf16[4,24,1024]{2,1,0:T(8,128)(2,1)S(1)}, u32[]{:S(2)}, u32[]{:S(2)}) collective-permute-start(bf16[4,24,1024]{2,1,0:T(8,128)(2,1)S(1)} %bitcast.69), channel_id=1, source_target_pairs={{2,0},{4,2},{6,4},{8,6},{10,8},{12,10},{14,12},{16,14},{18,16},{20... | collective-permute-start | bytes 589832 | tf_op jit(solution)/shard_map/ppermute | solution.py:19
  192.9 33.0 %copy-start.2 = (bf16[128,24,1024]{2,1,0:T(8,128)(2,1)}, bf16[128,24,1024]{2,1,0:T(8,128)(2,1)S(1)}, u32[]{:S(2)}) copy-start(bf16[128,24,1024]{2,1,0:T(8,128)(2,1)S(1)} %broadcast_select_fusion.1) | copy-start | bytes 18874372
  193.0 7.2 %copy-start.5 = (bf16[128,16,24]{2,1,0:T(8,128)(2,1)S(1)}, bf16[128,16,24]{2,1,0:T(8,128)(2,1)}, u32[]{:S(2)}) copy-start(bf16[128,16,24]{2,1,0:T(8,128)(2,1)} %copy.43) | copy-start | bytes 294916
  200.2 4.3 %copy-start.6 = (bf16[128,16,24]{2,1,0:T(8,128)(2,1)S(1)}, bf16[128,16,24]{2,1,0:T(8,128)(2,1)}, u32[]{:S(2)}) copy-start(bf16[128,16,24]{2,1,0:T(8,128)(2,1)} %copy.45) | copy-start | bytes 294916
  208.8 4.3 %copy-start.7 = (bf16[128,16,24]{2,1,0:T(8,128)(2,1)S(1)}, bf16[128,16,24]{2,1,0:T(8,128)(2,1)}, u32[]{:S(2)}) copy-start(bf16[128,16,24]{2,1,0:T(8,128)(2,1)} %copy.53) | copy-start | bytes 294916
  213.1 4.3 %copy-start.8 = (bf16[128,16,24]{2,1,0:T(8,128)(2,1)S(1)}, bf16[128,16,24]{2,1,0:T(8,128)(2,1)}, u32[]{:S(2)}) copy-start(bf16[128,16,24]{2,1,0:T(8,128)(2,1)} %copy.55) | copy-start | bytes 294916
  217.4 4.3 %copy-start.9 = (bf16[128,16,24]{2,1,0:T(8,128)(2,1)S(1)}, bf16[128,16,24]{2,1,0:T(8,128)(2,1)}, u32[]{:S(2)}) copy-start(bf16[128,16,24]{2,1,0:T(8,128)(2,1)} %copy.57) | copy-start | bytes 294916
  230.2 55.2 %copy-start.1 = (f32[256,256]{1,0:T(8,128)S(1)}, f32[256,256]{1,0:T(8,128)}, u32[]{:S(2)}) copy-start(f32[256,256]{1,0:T(8,128)} %param.11) | copy-start | bytes 786436
Sparse Core Ops, SparseCore 0:
  9.5 11.4 all-gather.1
  33.7 115.1 all-reduce.1
  277.9 5.9 reduce-scatter.3
where the time goes:
time: 293 us; the launch traced here: 292 us
  waiting for transfers between devices  125 us (43%)
  matrix products  94 us (32%)
  local copies, waits for them, and re-layouts  45.5 us (16%)
  between operations  14.1 us (5%)
  other arithmetic  7.78 us (3%)
  starting transfers between devices  5.79 us (2%)
    psum x1, waiting for transfers between devices, local(): inner_products = lax.psum(inner_products, 'row')  115 us
    dot_general x1, matrix products, local(): jnp.einsum('ain,ajn->aij', weighted, rounded, preferred_element_type=jnp....  46.4 us
    dot_general x8, matrix products, local(): jnp.einsum('aij,ajn->ain', blocks, neighbours, preferred_element_type=jnp...  34.3 us
    gather x1, local copies, waits for them, and re-layouts, local(): jnp.take(vectors, row_index.reshape(-1), axis=0, mode='fill', fill_value=0)  18.7 us
    unnamed x42, local copies, waits for them, and re-layouts  16.4 us
    select_n x9, local copies, waits for them, and re-layouts, local(): jnp.where(block_present[:, relative, None, None] > 0, blocks, jnp.zeros_l...  7.69 us
    unnamed x4, waiting for transfers between devices  6.78 us
  transfers between devices with their start and end apart: 5, of which 3 were waited for; matrix products, arithmetic and copies ran while one was open for 13% of the time, Pallas kernels for 0%

commit v1 on v0

v1 whole, which is shorter than its diff:
```python
import functools

import jax
import jax.numpy as jnp
import numpy as np
from jax import lax
from jax.experimental import pallas as pl
from jax.experimental.pallas import tpu as pltpu
from jax.sharding import PartitionSpec as P

NPMAX = 16
BMAX = 24
K = 9
RIM = (K - 1) // 2
HALO = RIM * BMAX
GROUP = 8
WIN = (GROUP + K - 1) * BMAX
F32 = jnp.float32
BF16 = jnp.bfloat16
MESH = pl.DeviceIdType.MESH


def mix_kernel(n, vec_hbm, panel_ref, factor_ref, cm_ref, spread_ref, fold_ref,
               mix_ref, pan_ref, halo_ref, band_ref,
               vec, part, got, load_sem, own_sem, pan_sems, halo_sems, inner_sems, mix_sems):
    row, col = lax.axis_index("row"), lax.axis_index("col")
    other = 1 - col
    up, down = lax.rem(row + 1, n), lax.rem(row + n - 1, n)
    rows = panel_ref.shape[0]
    half = panel_ref.shape[1]
    slab = mix_ref.shape[0] // n

    loads = pltpu.make_async_copy(vec_hbm, vec, load_sem)
    loads.start()
    own = pltpu.make_async_copy(panel_ref, pan_ref.at[col, pl.ds(HALO, rows)], own_sem)
    own.start()

    barrier = pltpu.get_barrier_semaphore()
    for step in range(1, n):
        peer = lax.rem(row + step, n)
        pl.semaphore_signal(barrier, inc=1, device_id=(peer, col), device_id_type=MESH)
    for peer in (row, up, down):
        pl.semaphore_signal(barrier, inc=1, device_id=(peer, other), device_id_type=MESH)
    pl.semaphore_wait(barrier, n - 1 + 3)

    def remote(src, dst, sems, slot, target):
        return pltpu.make_async_remote_copy(
            src_ref=src, dst_ref=dst, send_sem=sems.at[(0,) + slot], recv_sem=sems.at[(1,) + slot],
            device_id=target, device_id_type=MESH)

    swap = remote(panel_ref, pan_ref.at[col, pl.ds(HALO, rows)], pan_sems, (0,), (row, other))
    swap.start()
    halos = []
    for side, target in ((0, up), (1, down)):
        src_at = rows - HALO if side == 0 else 0
        dst_at = 0 if side == 0 else HALO + rows
        for where in (0, 1):
            to = col if where == 0 else other
            halos.append(remote(panel_ref.at[pl.ds(src_at, HALO)], pan_ref.at[col, pl.ds(dst_at, HALO)],
                                pan_sems, (1 + 2 * side + where,), (target, to)))
        halos.append(remote(vec_hbm.at[pl.ds(src_at, HALO)], halo_ref.at[side], halo_sems, (side,), (target, col)))
    loads.wait()

    def product(which, source):
        piece = lax.dot_general(source, vec[...], (((0,), (0,)), ((), ())), preferred_element_type=F32)
        part[which] = piece.T.astype(BF16)

    def inner_copy(which, step):
        peer = lax.rem(row + step, n)
        return remote(part.at[which, pl.ds(pl.multiple_of(peer * slab, slab), slab)],
                      got.at[which, step], inner_sems, (which, step), (peer, col))

    product(col, panel_ref[...])
    for step in range(1, n):
        inner_copy(col, step).start()
    swap.wait_recv()
    product(other, pan_ref[other, HALO:HALO + rows, :])
    for step in range(1, n):
        inner_copy(other, step).start()
    for copy in halos:
        copy.start()

    atoms = cm_ref.shape[1]

    def band_step(t, carry):
        acc = None
        lane = lax.broadcasted_iota(jnp.int32, (2 * GROUP * NPMAX, fold_ref.shape[1]), 1)
        for k in range(K):
            block = cm_ref[k, pl.ds(pl.multiple_of(t * 2 * GROUP, 2 * GROUP), 2 * GROUP), :].astype(F32)
            block = jnp.broadcast_to(block[:, None, :], (2 * GROUP, NPMAX, block.shape[1]))
            block = block.reshape(2 * GROUP * NPMAX, block.shape[2]) * spread_ref[...]
            folded = jnp.dot(block.astype(BF16), fold_ref[...], preferred_element_type=F32)
            inside = (lane >= k * BMAX) & (lane < (k + 1) * BMAX)
            acc = jnp.where(inside, folded, 0.0 if acc is None else acc)
        acc = jnp.concatenate([acc, jnp.zeros((acc.shape[0], WIN - acc.shape[1]), F32)], axis=1)
        for g in range(2):
            pieces = []
            for a in range(GROUP):
                at = (g * GROUP + a) * NPMAX
                piece = acc[at:at + NPMAX]
                pieces.append(piece if a == 0 else pltpu.roll(piece, a * BMAX, 1))
            band_ref[2 * t + g] = jnp.concatenate(pieces, axis=0).astype(BF16)
        return carry

    lax.fori_loop(0, atoms // (2 * GROUP), band_step, 0)

    mine = pl.ds(pl.multiple_of(row * slab, slab), slab)
    sums = []
    for which in (0, 1):
        sums.append(part[which, mine, :].astype(F32))
    for step in range(1, n):
        for which in (0, 1):
            inner_copy(which, step).wait_recv()
            sums[which] = sums[which] + got[which, step].astype(F32)
    inner = jnp.concatenate(sums, axis=1)
    mixed = jnp.dot(inner, factor_ref[...], precision=lax.Precision.HIGHEST, preferred_element_type=F32)
    mix_ref[mine, :] = mixed.astype(BF16)

    def mix_copy(step):
        peer = lax.rem(row + step, n)
        return remote(mix_ref.at[mine], mix_ref.at[mine], mix_sems, (step,), (peer, col))

    for step in range(1, n):
        mix_copy(step).start()
    own.wait()
    swap.wait_send()
    for copy in halos:
        copy.wait()
    for step in range(1, n):
        for which in (0, 1):
            inner_copy(which, step).wait_send()
    for step in range(1, n):
        mix_copy(step).wait()


def density_kernel(tiles, starts_ref, vin_ref, halo_ref, pan_ref, mix_ref, band_ref, weight_ref, expand_ref,
                   vec_ref, den_ref, ext, padded):
    step = pl.program_id(0)
    tile = vin_ref.shape[0]
    rows = tile * tiles

    def rotate(at, count, columns):
        panel = jnp.concatenate([pan_ref[0, pl.ds(at, count), :], pan_ref[1, pl.ds(at, count), :]], axis=1)
        update = lax.dot_general(panel, mix_ref[...], (((1,), (1,)), ((), ())), preferred_element_type=F32)
        return (columns.astype(F32) - update).astype(BF16)

    def keep(at, count, values):
        values = values.astype(F32)
        for c in range(ext.shape[0]):
            ext[c, pl.ds(at, count), :] = values[:, c * 128:(c + 1) * 128]

    @pl.when(step == 0)
    def _():
        keep(0, HALO, rotate(0, HALO, halo_ref[0]))
        keep(HALO + rows, HALO, rotate(HALO + rows, HALO, halo_ref[1]))
        spare = ext.shape[1] - 2 * HALO - rows
        ext[:, 2 * HALO + rows:, :] = jnp.zeros((ext.shape[0], spare, ext.shape[2]), F32)

    @pl.when(step < tiles)
    def _():
        at = pl.multiple_of(HALO + step * tile, 16)
        fresh = rotate(at, tile, vin_ref[...])
        vec_ref[...] = fresh
        keep(at, tile, fresh)

    @pl.when(step >= tiles)
    def _():
        j = step - tiles
        for pair in range(GROUP // 2):
            at = pl.multiple_of((j * GROUP + 2 * pair) * BMAX, 16)
            begins = [starts_ref[j * GROUP + 2 * pair + e] for e in (0, 1)]
            for c in range(ext.shape[0]):
                both = [ext[c, pl.ds(begin, BMAX), :] for begin in begins]
                both = jnp.concatenate(both, axis=0).astype(BF16)
                padded[pl.ds(at, 2 * BMAX), c * 128:(c + 1) * 128] = both

    @pl.when(step > tiles)
    def _():
        g = step - tiles - 1
        window = padded[pl.ds(pl.multiple_of(g * GROUP * BMAX, 16), WIN), :]
        rounded = jnp.dot(band_ref[0], window, preferred_element_type=F32).astype(BF16)
        weighted = (rounded.astype(F32) * weight_ref[...]).astype(BF16)
        full = lax.dot_general(weighted, rounded, (((1,), (1,)), ((), ())), preferred_element_type=F32)
        shape = full.shape
        own = lax.broadcasted_iota(jnp.int32, shape, 0) >> 4 == lax.broadcasted_iota(jnp.int32, shape, 1) >> 4
        full = jnp.where(own, full, 0.0)
        wide = jnp.dot(full, expand_ref[...], precision=lax.Precision.HIGHEST, preferred_element_type=F32)
        shape = wide.shape
        pick = (lax.broadcasted_iota(jnp.int32, shape, 0) & 15) == lax.broadcasted_iota(jnp.int32, shape, 1) >> 4
        wide = jnp.where(pick, wide, 0.0)
        den_ref[...] = wide.reshape(GROUP, NPMAX, wide.shape[1]).sum(axis=1)


def local(vectors_in, panel, factor, atom_basis, proj_count, coupling, block_present, occ_mask, occ_weight):
    n = lax.axis_size("row")
    rows, cols = vectors_in.shape
    half = panel.shape[1]
    npan = factor.shape[0]
    counts = atom_basis[0]
    atoms = counts.shape[0]
    groups = atoms // GROUP
    upward = [(i, (i + 1) % n) for i in range(n)]
    downward = [(j, i) for i, j in upward]
    before = lax.ppermute(counts[atoms - RIM:], "row", upward)
    after = lax.ppermute(counts[:RIM], "row", downward)
    counts_ext = jnp.concatenate([before, counts, after])
    starts = jnp.cumsum(counts_ext) - counts_ext + (HALO - jnp.sum(before))

    reach = jnp.stack([counts_ext[k:k + atoms] for k in range(K)], axis=0)
    reach = jnp.where(block_present.T > 0, reach, 0)
    lane = np.arange(NPMAX * BMAX)
    slot = jnp.asarray(lane % BMAX, jnp.int32)
    proj = jnp.asarray(lane // BMAX, jnp.int32)
    keep = (slot[None, None, :] < reach[:, :, None]) & (proj[None, None, :] < proj_count[None, :, None])
    cm = jnp.where(keep, jnp.swapaxes(coupling, 0, 1), jnp.zeros((), BF16))

    spread = jnp.asarray((lane[None, :] // BMAX) == (np.arange(2 * GROUP * NPMAX)[:, None] % NPMAX), F32)
    wide = np.arange(256)
    fold = jnp.asarray(((lane[:, None] % BMAX) == (wide[None, :] % BMAX)) & (wide[None, :] < K * BMAX), BF16)
    expand = jnp.asarray(
        (np.arange(GROUP * NPMAX)[:, None] % NPMAX) == (np.arange(NPMAX * NPMAX)[None, :] % NPMAX), F32)

    vmem = pl.BlockSpec(memory_space=pltpu.VMEM)
    slab = cols // n
    ext_rows = rows + 2 * HALO
    mix, pan, halo, band = pl.pallas_call(
        functools.partial(mix_kernel, n),
        out_shape=(
            jax.ShapeDtypeStruct((cols, npan), BF16),
            jax.ShapeDtypeStruct((2, ext_rows, half), BF16),
            jax.ShapeDtypeStruct((2, HALO, cols), BF16),
            jax.ShapeDtypeStruct((groups, GROUP * NPMAX, WIN), BF16),
        ),
        in_specs=[pl.BlockSpec(memory_space=pl.ANY)] + [vmem] * 5,
        out_specs=(vmem,) * 4,
        scratch_shapes=[
            pltpu.VMEM((rows, cols), BF16),
            pltpu.VMEM((2, cols, half), BF16),
            pltpu.VMEM((2, n, slab, half), BF16),
            pltpu.SemaphoreType.DMA,
            pltpu.SemaphoreType.DMA,
            pltpu.SemaphoreType.DMA((2, 5)),
            pltpu.SemaphoreType.DMA((2, 2)),
            pltpu.SemaphoreType.DMA((2, 2, n)),
            pltpu.SemaphoreType.DMA((2, n)),
        ],
        compiler_params=pltpu.CompilerParams(collective_id=0, has_side_effects=True, vmem_limit_bytes=40 << 20),
        cost_estimate=pl.CostEstimate(flops=8 * 10**9, bytes_accessed=10 << 20, transcendentals=0),
    )(vectors_in, panel, factor, cm, spread, fold)

    weights = occ_mask.astype(F32) * occ_weight / (cols * lax.axis_size("col"))
    tiles = 8
    tile = rows // tiles
    const = lambda *shape: pl.BlockSpec(shape, lambda s, st: (0,) * len(shape))
    vectors, partial = pl.pallas_call(
        functools.partial(density_kernel, tiles),
        out_shape=(
            jax.ShapeDtypeStruct((rows, cols), BF16),
            jax.ShapeDtypeStruct((atoms, NPMAX * NPMAX), F32),
        ),
        grid_spec=pltpu.PrefetchScalarGridSpec(
            num_scalar_prefetch=1,
            grid=(tiles + groups + 1,),
            in_specs=[
                pl.BlockSpec((tile, cols), lambda s, st: (jnp.minimum(s, tiles - 1), 0)),
                const(2, HALO, cols),
                const(2, ext_rows, half),
                const(cols, npan),
                pl.BlockSpec((1, GROUP * NPMAX, WIN), lambda s, st: (jnp.maximum(s - tiles - 1, 0), 0, 0)),
                const(1, cols),
                const(GROUP * NPMAX, NPMAX * NPMAX),
            ],
            out_specs=[
                pl.BlockSpec((tile, cols), lambda s, st: (jnp.minimum(s, tiles - 1), 0)),
                pl.BlockSpec((GROUP, NPMAX * NPMAX), lambda s, st: (jnp.maximum(s - tiles - 1, 0), 0)),
            ],
            scratch_shapes=[
                pltpu.VMEM((cols // 128, ext_rows + BMAX, 128), F32),
                pltpu.VMEM(((atoms + 2 * RIM) * BMAX, cols), BF16),
            ],
        ),
        compiler_params=pltpu.CompilerParams(vmem_limit_bytes=48 << 20),
        cost_estimate=pl.CostEstimate(flops=6 * 10**9, bytes_accessed=10 << 20, transcendentals=0),
    )(starts, vectors_in, halo, pan, mix, band, weights[None, :], expand)

    ncol = lax.axis_size("col")
    share = atoms // ncol
    col = lax.axis_index("col")
    density = lax.dynamic_slice_in_dim(partial, col * share, share, 0)
    for step in range(1, ncol):
        sent = lax.dynamic_slice_in_dim(partial, lax.rem(col + step, ncol) * share, share, 0)
        density = density + lax.ppermute(sent, "col", [(i, (i + step) % ncol) for i in range(ncol)])
    return (vectors, density)


def solution(mesh):
    placed = (
        P("row", "col"),
        P("row", "col"),
        P(),
        P("row", None),
        P("row"),
        P("row", None, None),
        P("row", None),
        P("col"),
        P("col"),
    )
    return jax.shard_map(
        local,
        mesh=mesh,
        in_specs=placed,
        out_specs=(P("row", "col"), P(("row", "col"), None)),
        check_vma=False,
    )
```

time: 293 us -> 80.7 us (0.28)
  the two profiles are of different devices: /device:TPU:0 before, /device:TPU:17 now
where the time goes in v1:
time: 80.7 us; the launch traced here: 80.2 us
  Pallas kernels  60.7 us (75%)
  other arithmetic  7.12 us (9%)
  starting transfers between devices  5.98 us (7%)
  local copies, waits for them, and re-layouts  4.03 us (5%)
  between operations  1.4 us (2%)
  waiting for transfers between devices  0.91 us (1%)
    pallas_call x1, Pallas kernels, local(): pl.pallas_call(functools.partial(mix_kernel, n), out_shape=(jax.ShapeDtyp...  36.7 us
    pallas_call x1, Pallas kernels, local(): pl.pallas_call(functools.partial(density_kernel, tiles), out_shape=(jax.S...  24.1 us
    ppermute x1, starting transfers between devices, local(): lax.ppermute(sent, 'col', [(i, (i + step) % ncol) for i in range(ncol)])  2.72 us
    unnamed x14, local copies, waits for them, and re-layouts  2.21 us
    ppermute x1, starting transfers between devices, local(): after = lax.ppermute(counts[:RIM], 'row', downward)  2.05 us
    select_n x1, other arithmetic, local(): cm = jnp.where(keep, jnp.swapaxes(coupling, 0, 1), jnp.zeros((), BF16))  1.62 us
  transfers between devices with their start and end apart: 3, of which 1 were waited for; matrix products, arithmetic and copies ran while one was open for 2% of the time, Pallas kernels for 0%

profile of v1, /device:TPU:17, one launch (start us, length us, event | category | flops | bytes accessed | tf_op | source)
XLA Modules:
  0.0 80.2 jit_solution(5220444704422806978)
XLA Ops:
  0.6 0.0 copy-start.3
  0.7 0.8 %slice_bitcast_fusion.9 = (s32[4]{0:T(128)S(1)}, s32[4]{0:T(128)S(1)}) fusion(s32[1,128]{1,0:T(1,128)} %param.17), kind=kLoop, calls=%fused_computation.22 | loop fusion | bytes 64 | tf_op jit(solution)/shard_map/slice | solution.py:204
  1.5 1.2 %collective-permute-start = (s32[4]{0:T(128)S(1)}, s32[4]{0:T(128)S(1)}, u32[]{:S(2)}, u32[]{:S(2)}) collective-permute-start(s32[4]{0:T(128)S(1)} %get-tuple-element.24), channel_id=1, source_target_pairs={{0,2},{2,4},{4,6},{6,8},{8,10},{10,12},{12,14},{14,16},{16,18},{18... | collective-permute-start | bytes 56 | tf_op jit(solution)/shard_map/ppermute | solution.py:204
  2.7 2.1 %collective-permute-start.1 = (s32[4]{0:T(128)S(1)}, s32[4]{0:T(128)S(1)}, u32[]{:S(2)}, u32[]{:S(2)}) collective-permute-start(s32[4]{0:T(128)S(1)} %get-tuple-element.25), channel_id=1, source_target_pairs={{2,0},{4,2},{6,4},{8,6},{10,8},{12,10},{14,12},{16,14},{18,16},{20... | collective-permute-start | bytes 56 | tf_op jit(solution)/shard_map/ppermute | solution.py:205
  4.8 0.8 broadcast_compare_fusion
  5.6 0.7 multiply_multiply_fusion
  6.3 0.7 pad_add_fusion
  7.0 0.3 reduce-window.9
  7.3 0.1 slice.58
  7.4 0.1 slice_reduce_fusion
  7.6 0.1 add_bitcast_fusion
  7.6 0.8 %pad_add_fusion.2 = (s32[132]{0:T(256)S(1)}, s32[132]{0:T(256)S(1)}) fusion(s32[4]{0:T(128)S(1)} %collective-permute-done.1, s32[128]{0:T(128)} %bitcast.32, s32[4]{0:T(128)S(1)} %collective-permute-done), kind=kLoop, calls=%fused_computation.7 | loop fusion | flops 264 | bytes 1600 | tf_op jit(solution)/shard_map/concatenate | solution.py:206
  8.4 0.1 slice_bitcast_fusion
  8.5 0.7 stack.35
  9.2 0.7 bitcast_select_fusion
  9.9 0.6 reduce_sum.9
  11.2 1.6 %and_select_fusion.cm_ref = bf16[9,128,384]{2,1,0:T(8,128)(2,1)S(1)} fusion(bf16[128,9,384]{2,0,1:T(8,128)(2,1)} %param.19, s32[9,128]{1,0:T(8,128)S(1)} %bitcast_select_fusion, s32[384]{0:T(512)} %constant.36.clone, pred[128,384]{1,0:T(8,128)(4,1)S(1)} %broadcast_compare_fusion), kind=kLoop, calls=%fused_computation | loop fusion | flops 1327104 | bytes 1824768 | tf_op jit(solution)/shard_map/jit(_where)/select_n | solution.py:215
  12.9 2.2 %copy-done = bf16[2048,1024]{1,0:T(8,128)(2,1)S(1)} copy-done((bf16[2048,1024]{1,0:T(8,128)(2,1)S(1)}, bf16[2048,1024]{1,0:T(8,128)(2,1)}, u32[]{:S(2)}) %copy-start) | copy-done | bytes 4194328
  15.1 36.7 %shard_map.149 = (bf16[1024,256]{1,0:T(8,128)(2,1)S(1)}, bf16[2,2240,128]{2,1,0:T(8,128)(2,1)S(1)}, bf16[2,96,1024]{2,1,0:T(8,128)(2,1)S(1)}, bf16[16,128,384]{2,1,0:T(8,128)(2,1)S(1)}) custom-call(bf16[2048,1024]{1,0:T(8,128)(2,1)S(1)} %copy-done, bf16[2048,128]{1,0:T(8,128)(2,1)S(1)} %copy-done.1, f32[256,256]{1,0:T(8,128)S(1)} %copy-done.2, ...), custom_call_target="tpu_custom_call" | custom-call | flops 8000000000 | bytes 10485760 | tf_op jit(solution)/shard_map/pallas_call | solution.py:226
  51.8 0.1 subtract_add_fusion.starts_ref
  51.9 24.1 %shard_map.150 = (bf16[2048,1024]{1,0:T(8,128)(2,1)}, f32[128,256]{1,0:T(8,128)S(1)}) custom-call(s32[136]{0:T(256)S(1)} %subtract_add_fusion.starts_ref, bf16[2048,1024]{1,0:T(8,128)(2,1)} %vin_ref.1, bf16[2,96,1024]{2,1,0:T(8,128)(2,1)S(1)} %get-tuple-element.8.halo_ref, bf16[2,2240,128]{2,1,0:T(8,128)(2,1)S(1)} %get-tuple-element.9.pan_ref, ...), custom_call_target="tpu_custom_call" | custom-call | flops 6000000000 | bytes 10485760 | tf_op jit(solution)/shard_map/pallas_call | solution.py:255
  75.9 2.7 %collective-permute-start.2 = (f32[64,256]{1,0:T(8,128)S(1)}, f32[64,256]{1,0:T(8,128)S(1)}, u32[]{:S(2)}, u32[]{:S(2)}) collective-permute-start(f32[64,256]{1,0:T(8,128)S(1)} %constant_dynamic-slice_fusion), channel_id=1, source_target_pairs={{0,1},{1,0},{2,3},{3,2},{4,5},{5,4},{6,7},{7,6},{8,9},{9,8},{10,11... | collective-permute-start | bytes 196616 | tf_op jit(solution)/shard_map/ppermute | solution.py:292
  78.6 0.9 %collective-permute-done.2 = f32[64,256]{1,0:T(8,128)S(1)} collective-permute-done((f32[64,256]{1,0:T(8,128)S(1)}, f32[64,256]{1,0:T(8,128)S(1)}, u32[]{:S(2)}, u32[]{:S(2)}) %collective-permute-start.2) | collective-permute-done | bytes 65568 | tf_op jit(solution)/shard_map/ppermute | solution.py:292
  79.5 0.6 dynamic-slice_add_fusion
  (17 shorter events, 0.1 us)
Async XLA Ops:
  0.6 12.2 %copy-start.3 = (f32[256,384]{1,0:T(8,128)S(1)}, f32[256,384]{1,0:T(8,128)}, u32[]{:S(2)}) copy-start(f32[256,384]{1,0:T(8,128)} %constant.38.clone.spread_ref) | copy-start | bytes 1179652
  0.6 12.2 %copy-start.4 = (bf16[384,256]{1,0:T(8,128)(2,1)S(1)}, bf16[384,256]{1,0:T(8,128)(2,1)}, u32[]{:S(2)}) copy-start(bf16[384,256]{1,0:T(8,128)(2,1)} %constant.39.clone.fold_ref) | copy-start | bytes 589828
  0.7 12.2 %copy-start.1 = (bf16[2048,128]{1,0:T(8,128)(2,1)S(1)}, bf16[2048,128]{1,0:T(8,128)(2,1)}, u32[]{:S(2)}) copy-start(bf16[2048,128]{1,0:T(8,128)(2,1)} %panel_ref.1) | copy-start | bytes 1572868
  0.7 12.2 %copy-start.2 = (f32[256,256]{1,0:T(8,128)S(1)}, f32[256,256]{1,0:T(8,128)}, u32[]{:S(2)}) copy-start(f32[256,256]{1,0:T(8,128)} %factor_ref.1) | copy-start | bytes 786436
  1.5 4.8 %collective-permute-start = (s32[4]{0:T(128)S(1)}, s32[4]{0:T(128)S(1)}, u32[]{:S(2)}, u32[]{:S(2)}) collective-permute-start(s32[4]{0:T(128)S(1)} %get-tuple-element.24), channel_id=1, source_target_pairs={{0,2},{2,4},{4,6},{6,8},{8,10},{10,12},{12,14},{14,16},{16,18},{18... | collective-permute-start | bytes 56 | tf_op jit(solution)/shard_map/ppermute | solution.py:204
  2.7 3.6 %collective-permute-start.1 = (s32[4]{0:T(128)S(1)}, s32[4]{0:T(128)S(1)}, u32[]{:S(2)}, u32[]{:S(2)}) collective-permute-start(s32[4]{0:T(128)S(1)} %get-tuple-element.25), channel_id=1, source_target_pairs={{2,0},{4,2},{6,4},{8,6},{10,8},{12,10},{14,12},{16,14},{18,16},{20... | collective-permute-start | bytes 56 | tf_op jit(solution)/shard_map/ppermute | solution.py:205
  12.9 2.2 %copy-start = (bf16[2048,1024]{1,0:T(8,128)(2,1)S(1)}, bf16[2048,1024]{1,0:T(8,128)(2,1)}, u32[]{:S(2)}) copy-start(bf16[2048,1024]{1,0:T(8,128)(2,1)} %vin_ref.1) | copy-start | bytes 12582916
  15.1 36.7 %copy-start.6 = (s32[1,128]{1,0:T(1,128)S(1)}, s32[1,128]{1,0:T(1,128)}, u32[]{:S(2)}) copy-start(s32[1,128]{1,0:T(1,128)} %param.17) | copy-start | bytes 1540
  15.1 36.8 %copy-start.5 = (f32[128,256]{1,0:T(8,128)S(1)}, f32[128,256]{1,0:T(8,128)}, u32[]{:S(2)}) copy-start(f32[128,256]{1,0:T(8,128)} %constant.40.clone.expand_ref) | copy-start | bytes 393220
  75.9 3.6 %collective-permute-start.2 = (f32[64,256]{1,0:T(8,128)S(1)}, f32[64,256]{1,0:T(8,128)S(1)}, u32[]{:S(2)}, u32[]{:S(2)}) collective-permute-start(f32[64,256]{1,0:T(8,128)S(1)} %constant_dynamic-slice_fusion), channel_id=1, source_target_pairs={{0,1},{1,0},{2,3},{3,2},{4,5},{5,4},{6,7},{7,6},{8,9},{9,8},{10,11... | collective-permute-start | bytes 196616 | tf_op jit(solution)/shard_map/ppermute | solution.py:292

commit v2 on v1

v2 whole, which is shorter than its diff:
```python
import functools

import jax
import jax.numpy as jnp
from jax import lax
from jax.experimental import pallas as pl
from jax.experimental.pallas import tpu as pltpu
from jax.sharding import PartitionSpec as P

NPMAX = 16
BMAX = 24
K = 9
RIM = (K - 1) // 2
HALO = RIM * BMAX
GROUP = 16
WIN = -(-(GROUP + K - 1) * BMAX // 128) * 128
FOLD = -(-K * BMAX // 128) * 128
TILES = 4
F32 = jnp.float32
BF16 = jnp.bfloat16
MESH = pl.DeviceIdType.MESH


def iota(rows, columns, axis):
    return lax.broadcasted_iota(jnp.int32, (rows, columns), axis)


def group_of(rows, columns, axis, size, most):
    small = (8, columns) if axis == 1 else (rows, 128)
    index = iota(*small, axis)
    group = jnp.zeros(small, jnp.int32)
    for edge in range(1, most):
        group = group + jnp.where(index >= edge * size, 1, 0)
    return jnp.tile(group, (rows // small[0], columns // small[1]))


def mix_kernel(n, vec_hbm, panel_ref, factor_ref, basis_ref, proj_ref, cm_ref, present_ref,
               mix_ref, pan_ref, halo_ref, band_ref, start_ref,
               vec, part, got, counts, limit, spread, fold, load_sem, own_sem, pan_sems, halo_sems, count_sems, inner_sems, mix_sems):
    row, col = lax.axis_index("row"), lax.axis_index("col")
    other = 1 - col
    up, down = lax.rem(row + 1, n), lax.rem(row + n - 1, n)
    rows = panel_ref.shape[0]
    half = panel_ref.shape[1]
    slab = mix_ref.shape[0] // n

    loads = pltpu.make_async_copy(vec_hbm, vec, load_sem)
    loads.start()
    own = pltpu.make_async_copy(panel_ref, pan_ref.at[col, pl.ds(HALO, rows)], own_sem)
    own.start()

    barrier = pltpu.get_barrier_semaphore()
    for step in range(1, n):
        peer = lax.rem(row + step, n)
        pl.semaphore_signal(barrier, inc=1, device_id=(peer, col), device_id_type=MESH)
    for peer in (row, up, down):
        pl.semaphore_signal(barrier, inc=1, device_id=(peer, other), device_id_type=MESH)
    pl.semaphore_wait(barrier, n - 1 + 3)

    def remote(src, dst, sems, slot, target):
        return pltpu.make_async_remote_copy(
            src_ref=src, dst_ref=dst, send_sem=sems.at[(0,) + slot], recv_sem=sems.at[(1,) + slot],
            device_id=target, device_id_type=MESH)

    swap = remote(panel_ref, pan_ref.at[col, pl.ds(HALO, rows)], pan_sems, (0,), (row, other))
    swap.start()
    count_copies = [
        remote(basis_ref, counts.at[side], count_sems, (side,), (target, col))
        for side, target in ((0, up), (1, down))
    ]
    for copy in count_copies:
        copy.start()
    halos = []
    for side, target in ((0, up), (1, down)):
        src_at = rows - HALO if side == 0 else 0
        dst_at = 0 if side == 0 else HALO + rows
        for where in (0, 1):
            to = col if where == 0 else other
            halos.append(remote(panel_ref.at[pl.ds(src_at, HALO)], pan_ref.at[col, pl.ds(dst_at, HALO)],
                                pan_sems, (1 + 2 * side + where,), (target, to)))
        halos.append(remote(vec_hbm.at[pl.ds(src_at, HALO)], halo_ref.at[side], halo_sems, (side,), (target, col)))
    loads.wait()

    def product(which, source):
        piece = lax.dot_general(source, vec[...], (((0,), (0,)), ((), ())), preferred_element_type=F32)
        part[which] = piece.T.astype(BF16)

    def inner_copy(which, step):
        peer = lax.rem(row + step, n)
        return remote(part.at[which, pl.ds(pl.multiple_of(peer * slab, slab), slab)],
                      got.at[which, step], inner_sems, (which, step), (peer, col))

    product(col, panel_ref[...])
    for step in range(1, n):
        inner_copy(col, step).start()
    swap.wait_recv()
    product(other, pan_ref[other, HALO:HALO + rows, :])
    for step in range(1, n):
        inner_copy(other, step).start()
    for copy in halos:
        copy.start()

    atoms = cm_ref.shape[1]
    wide = cm_ref.shape[2]
    spread[...] = jnp.where(group_of(GROUP * NPMAX, wide, 1, BMAX, NPMAX) == (iota(GROUP * NPMAX, wide, 0) & 15),
                            1.0, 0.0)
    fold_slot = iota(wide, FOLD, 1) - BMAX * group_of(wide, FOLD, 1, BMAX, K)
    fold_from = iota(wide, FOLD, 0) - BMAX * group_of(wide, FOLD, 0, BMAX, NPMAX)
    fold[...] = jnp.where((fold_slot == fold_from) & (iota(wide, FOLD, 1) < K * BMAX), 1.0, 0.0).astype(BF16)
    for copy in count_copies:
        copy.wait_recv()
    here = basis_ref[...].astype(F32)
    prev, post = counts[0].astype(F32), counts[1].astype(F32)
    lower = jnp.where(iota(atoms, atoms, 0) < iota(atoms, atoms, 1), 1.0, 0.0).astype(BF16)
    table = jnp.concatenate([prev, here, post, jnp.zeros((5, atoms), F32)], axis=0).astype(BF16)
    first = jnp.dot(table, lower, preferred_element_type=F32).astype(jnp.int32)
    start_ref[...] = first + (HALO - rows) + rows * iota(8, atoms, 0)
    lines = []
    at = iota(1, atoms, 1)
    for k in range(K):
        d = k - RIM
        near = here
        if d != 0:
            turn = (-d) % atoms
            inside = (at + d >= 0) & (at + d < atoms)
            near = jnp.where(inside, pltpu.roll(here, turn, 1), pltpu.roll(prev if d < 0 else post, turn, 1))
        lines.append(jnp.where(present_ref[k:k + 1, :] > 0, near, 0.0))
    lines.append(proj_ref[...].astype(F32))
    lines.append(jnp.zeros((atoms - K - 1, atoms), F32))
    limit[...] = jnp.concatenate(lines, axis=0).T

    lane = iota(GROUP, FOLD, 1)
    in_k = group_of(GROUP, FOLD, 1, BMAX, K)
    slot = (lane - BMAX * in_k).astype(F32)

    def band_step(t, carry):
        chunk = pl.ds(pl.multiple_of(t * GROUP, GROUP), GROUP)
        bounds = limit[chunk, :]
        reach = jnp.zeros((GROUP, FOLD), F32)
        for k in range(K):
            reach = jnp.where(in_k == k, bounds[:, k:k + 1], reach)
        kept = jnp.where(slot < reach, 1.0, 0.0)
        kept = jnp.broadcast_to(kept[:, None, :], (GROUP, NPMAX, FOLD)).reshape(GROUP * NPMAX, FOLD)
        most = jnp.broadcast_to(bounds[:, K:K + 1], (GROUP, FOLD))
        most = jnp.broadcast_to(most[:, None, :], (GROUP, NPMAX, FOLD)).reshape(GROUP * NPMAX, FOLD)
        valid = (kept > 0.5) & ((iota(GROUP * NPMAX, FOLD, 0) & 15).astype(F32) < most)
        which_k = group_of(GROUP * NPMAX, FOLD, 1, BMAX, K)
        acc = jnp.zeros((GROUP * NPMAX, FOLD), F32)
        for k in range(K):
            block = cm_ref[k, chunk, :].astype(F32)
            block = jnp.broadcast_to(block[:, None, :], (GROUP, NPMAX, wide)).reshape(GROUP * NPMAX, wide)
            folded = jnp.dot((block * spread[...]).astype(BF16), fold[...], preferred_element_type=F32)
            acc = jnp.where(which_k == k, folded, acc)
        acc = jnp.where(valid, acc, 0.0)
        acc = jnp.concatenate([acc, jnp.zeros((acc.shape[0], WIN - FOLD), F32)], axis=1)
        pieces = []
        for a in range(GROUP):
            piece = acc[a * NPMAX:(a + 1) * NPMAX]
            pieces.append(piece if a == 0 else pltpu.roll(piece, a * BMAX, 1))
        band_ref[t] = jnp.concatenate(pieces, axis=0).astype(BF16)
        return carry

    lax.fori_loop(0, atoms // GROUP, band_step, 0)

    mine = pl.ds(pl.multiple_of(row * slab, slab), slab)
    sums = []
    for which in (0, 1):
        sums.append(part[which, mine, :].astype(F32))
    for step in range(1, n):
        for which in (0, 1):
            inner_copy(which, step).wait_recv()
            sums[which] = sums[which] + got[which, step].astype(F32)
    inner = jnp.concatenate(sums, axis=1)
    mixed = jnp.dot(inner, factor_ref[...], precision=lax.Precision.HIGHEST, preferred_element_type=F32)
    mix_ref[mine, :] = mixed.astype(BF16)

    def mix_copy(step):
        peer = lax.rem(row + step, n)
        return remote(mix_ref.at[mine], mix_ref.at[mine], mix_sems, (step,), (peer, col))

    for step in range(1, n):
        mix_copy(step).start()
    own.wait()
    swap.wait_send()
    for copy in count_copies:
        copy.wait_send()
    for copy in halos:
        copy.wait()
    for step in range(1, n):
        for which in (0, 1):
            inner_copy(which, step).wait_send()
    for step in range(1, n):
        mix_copy(step).wait()


def density_kernel(starts_ref, vin_ref, halo_ref, pan_ref, mix_ref, band_ref, mask_ref, occ_ref,
                   vec_ref, den_ref, ext, padded, mixing, weight, *, column_total):
    step = pl.program_id(0)
    tile = vin_ref.shape[0]
    rows = tile * TILES
    atoms = (padded.shape[0] - (WIN - (GROUP + K - 1) * BMAX)) // BMAX - 2 * RIM

    def rotate(at, count, columns):
        panel = jnp.concatenate([pan_ref[0, pl.ds(at, count), :], pan_ref[1, pl.ds(at, count), :]], axis=1)
        update = jnp.dot(panel, mixing[...], preferred_element_type=F32)
        return (columns.astype(F32) - update).astype(BF16)

    def keep(at, count, values):
        values = values.astype(F32)
        for c in range(ext.shape[0]):
            ext[c, pl.ds(at, count), :] = values[:, c * 128:(c + 1) * 128]

    def gather(atom, count):
        for pair in range(count // 2):
            at = pl.multiple_of((atom + 2 * pair) * BMAX, 16)
            begins = []
            for e in (0, 1):
                flat = atom + 2 * pair + e + atoms - RIM
                begins.append(starts_ref[lax.div(flat, atoms), lax.rem(flat, atoms)])
            for c in range(ext.shape[0]):
                both = [ext[c, pl.ds(begin, BMAX), :] for begin in begins]
                both = jnp.concatenate(both, axis=0).astype(BF16)
                padded[pl.ds(at, 2 * BMAX), c * 128:(c + 1) * 128] = both

    @pl.when(step == 0)
    def _():
        mixing[...] = mix_ref[...].T
        weight[...] = mask_ref[...].astype(F32) * occ_ref[...] / column_total
        keep(0, HALO, rotate(0, HALO, halo_ref[0]))
        keep(HALO + rows, HALO, rotate(HALO + rows, HALO, halo_ref[1]))
        spare = ext.shape[1] - 2 * HALO - rows
        ext[:, 2 * HALO + rows:, :] = jnp.zeros((ext.shape[0], spare, ext.shape[2]), F32)
        used = (atoms + 2 * RIM) * BMAX
        padded[used:, :] = jnp.zeros((padded.shape[0] - used, padded.shape[1]), BF16)

    @pl.when(step < TILES)
    def _():
        at = pl.multiple_of(HALO + step * tile, 16)
        fresh = rotate(at, tile, vin_ref[...])
        vec_ref[...] = fresh
        keep(at, tile, fresh)

    @pl.when(step == TILES - 1)
    def _():
        gather(0, 2 * RIM)

    @pl.when(step >= TILES)
    def _():
        g = step - TILES
        gather(g * GROUP + 2 * RIM, GROUP)
        window = padded[pl.ds(pl.multiple_of(g * GROUP * BMAX, 16), WIN), :]
        rounded = jnp.dot(band_ref[0], window, preferred_element_type=F32).astype(BF16)
        weighted = (rounded.astype(F32) * weight[...]).astype(BF16)
        full = lax.dot_general(weighted, rounded, (((1,), (1,)), ((), ())), preferred_element_type=F32)
        shape = full.shape
        full = jnp.where(iota(*shape, 0) >> 4 == iota(*shape, 1) >> 4, full, 0.0)
        expand = jnp.where((iota(shape[1], NPMAX * NPMAX, 0) & 15) == (iota(shape[1], NPMAX * NPMAX, 1) & 15),
                           1.0, 0.0).astype(BF16)
        spreads = 0.0
        for _ in range(3):
            top = full.astype(BF16)
            spreads = spreads + jnp.dot(top, expand, preferred_element_type=F32)
            full = full - top.astype(F32)
        shape = spreads.shape
        spreads = jnp.where((iota(*shape, 0) & 15) == iota(*shape, 1) >> 4, spreads, 0.0)
        den_ref[...] = spreads.reshape(GROUP, NPMAX, shape[1]).sum(axis=1)


def local(vectors_in, panel, factor, atom_basis, proj_count, coupling, block_present, occ_mask, occ_weight):
    n = lax.axis_size("row")
    rows, cols = vectors_in.shape
    half = panel.shape[1]
    npan = factor.shape[0]
    atoms = atom_basis.shape[1]
    groups = atoms // GROUP
    vmem = pl.BlockSpec(memory_space=pltpu.VMEM)
    slab = cols // n
    ext_rows = rows + 2 * HALO
    mix, pan, halo, band, starts = pl.pallas_call(
        functools.partial(mix_kernel, n),
        out_shape=(
            jax.ShapeDtypeStruct((cols, npan), BF16),
            jax.ShapeDtypeStruct((2, ext_rows, half), BF16),
            jax.ShapeDtypeStruct((2, HALO, cols), BF16),
            jax.ShapeDtypeStruct((groups, GROUP * NPMAX, WIN), BF16),
            jax.ShapeDtypeStruct((8, atoms), jnp.int32),
        ),
        in_specs=[pl.BlockSpec(memory_space=pltpu.HBM)] + [vmem] * 6,
        out_specs=(vmem,) * 5,
        scratch_shapes=[
            pltpu.VMEM((rows, cols), BF16),
            pltpu.VMEM((2, cols, half), BF16),
            pltpu.VMEM((2, n, slab, half), BF16),
            pltpu.VMEM((2, 1, atoms), jnp.int32),
            pltpu.VMEM((atoms, atoms), F32),
            pltpu.VMEM((GROUP * NPMAX, NPMAX * BMAX), F32),
            pltpu.VMEM((NPMAX * BMAX, FOLD), BF16),
            pltpu.SemaphoreType.DMA,
            pltpu.SemaphoreType.DMA,
            pltpu.SemaphoreType.DMA((2, 5)),
            pltpu.SemaphoreType.DMA((2, 2)),
            pltpu.SemaphoreType.DMA((2, 2)),
            pltpu.SemaphoreType.DMA((2, 2, n)),
            pltpu.SemaphoreType.DMA((2, n)),
        ],
        compiler_params=pltpu.CompilerParams(collective_id=0, has_side_effects=True, vmem_limit_bytes=40 << 20),
        cost_estimate=pl.CostEstimate(flops=8 * 10**9, bytes_accessed=10 << 20, transcendentals=0),
    )(vectors_in, panel, factor, atom_basis, proj_count[None, :], jnp.swapaxes(coupling, 0, 1), block_present.T)

    tile = rows // TILES
    const = lambda *shape: pl.BlockSpec(shape, lambda s, st: (0,) * len(shape))
    vectors, partial = pl.pallas_call(
        functools.partial(density_kernel, column_total=cols * lax.axis_size("col")),
        out_shape=(
            jax.ShapeDtypeStruct((rows, cols), BF16),
            jax.ShapeDtypeStruct((atoms, NPMAX * NPMAX), F32),
        ),
        grid_spec=pltpu.PrefetchScalarGridSpec(
            num_scalar_prefetch=1,
            grid=(TILES + groups,),
            in_specs=[
                pl.BlockSpec((tile, cols), lambda s, st: (jnp.minimum(s, TILES - 1), 0)),
                const(2, HALO, cols),
                const(2, ext_rows, half),
                const(cols, npan),
                pl.BlockSpec((1, GROUP * NPMAX, WIN), lambda s, st: (jnp.maximum(s - TILES, 0), 0, 0)),
                const(1, cols),
                const(1, cols),
            ],
            out_specs=[
                pl.BlockSpec((tile, cols), lambda s, st: (jnp.minimum(s, TILES - 1), 0)),
                pl.BlockSpec((GROUP, NPMAX * NPMAX), lambda s, st: (jnp.maximum(s - TILES, 0), 0)),
            ],
            scratch_shapes=[
                pltpu.VMEM((cols // 128, ext_rows + BMAX, 128), F32),
                pltpu.VMEM(((atoms + 2 * RIM) * BMAX + WIN - (GROUP + K - 1) * BMAX, cols), BF16),
                pltpu.VMEM((npan, cols), BF16),
                pltpu.VMEM((1, cols), F32),
            ],
        ),
        compiler_params=pltpu.CompilerParams(vmem_limit_bytes=48 << 20),
        cost_estimate=pl.CostEstimate(flops=6 * 10**9, bytes_accessed=10 << 20, transcendentals=0),
    )(starts, vectors_in, halo, pan, mix, band, occ_mask[None, :], occ_weight[None, :])

    ncol = lax.axis_size("col")
    share = atoms // ncol
    col = lax.axis_index("col")
    density = lax.dynamic_slice_in_dim(partial, col * share, share, 0)
    for step in range(1, ncol):
        sent = lax.dynamic_slice_in_dim(partial, lax.rem(col + step, ncol) * share, share, 0)
        density = density + lax.ppermute(sent, "col", [(i, (i + step) % ncol) for i in range(ncol)])
    return (vectors, density)


def solution(mesh):
    placed = (
        P("row", "col"),
        P("row", "col"),
        P(),
        P("row", None),
        P("row"),
        P("row", None, None),
        P("row", None),
        P("col"),
        P("col"),
    )
    return jax.shard_map(
        local,
        mesh=mesh,
        in_specs=placed,
        out_specs=(P("row", "col"), P(("row", "col"), None)),
        check_vma=False,
    )
```

time: 80.7 us -> 64.7 us (0.80)
  the two profiles are of different devices: /device:TPU:17 before, /device:TPU:27 now
where the time goes in v2:
time: 64.7 us; the launch traced here: 64.3 us
  Pallas kernels  52.4 us (81%)
  local copies, waits for them, and re-layouts  7.36 us (11%)
  starting transfers between devices  2.26 us (3%)
  waiting for transfers between devices  0.9 us (1%)
  between operations  0.69 us (1%)
    pallas_call x1, Pallas kernels, local(): pl.pallas_call(functools.partial(mix_kernel, n), out_shape=(jax.ShapeDtyp...  35.1 us
    pallas_call x1, Pallas kernels, local(): pl.pallas_call(functools.partial(density_kernel, column_total=cols * lax....  17.4 us
    unnamed x18, local copies, waits for them, and re-layouts  7.35 us
    ppermute x1, starting transfers between devices, local(): lax.ppermute(sent, 'col', [(i, (i + step) % ncol) for i in range(ncol)])  2.26 us
  transfers between devices with their start and end apart: 1, of which 1 were waited for; matrix products, arithmetic and copies ran while one was open for 0% of the time, Pallas kernels for 0%

profile of v2, /device:TPU:27, one launch (start us, length us, event | category | flops | bytes accessed | tf_op | source)
XLA Modules:
  0.0 64.3 jit_solution(17806903451795858585)
XLA Ops:
  0.6 0.0 copy-start
  0.7 2.2 %copy-done = bf16[2048,1024]{1,0:T(8,128)(2,1)S(1)} copy-done((bf16[2048,1024]{1,0:T(8,128)(2,1)S(1)}, bf16[2048,1024]{1,0:T(8,128)(2,1)}, u32[]{:S(2)}) %copy-start) | copy-done | bytes 4194328
  2.8 0.0 copy-start.1
  2.8 1.2 %copy-done.1 = bf16[128,9,384]{2,0,1:T(8,128)(2,1)S(1)} copy-done((bf16[128,9,384]{2,0,1:T(8,128)(2,1)S(1)}, bf16[128,9,384]{2,0,1:T(8,128)(2,1)}, u32[]{:S(2)}) %copy-start.1) | copy-done | bytes 884760
  4.0 0.0 copy-start.2
  4.0 1.0 %copy-done.2 = bf16[2048,128]{1,0:T(8,128)(2,1)S(1)} copy-done((bf16[2048,128]{1,0:T(8,128)(2,1)S(1)}, bf16[2048,128]{1,0:T(8,128)(2,1)}, u32[]{:S(2)}) %copy-start.2) | copy-done | bytes 524312
  5.0 0.0 copy-start.3
  5.0 0.9 %copy-done.3 = f32[256,256]{1,0:T(8,128)S(1)} copy-done((f32[256,256]{1,0:T(8,128)S(1)}, f32[256,256]{1,0:T(8,128)}, u32[]{:S(2)}) %copy-start.3) | copy-done | bytes 262168
  6.0 0.0 copy-start.4
  6.0 0.7 %copy-done.4 = s32[128,9]{0,1:T(8,128)S(1)} copy-done((s32[128,9]{0,1:T(8,128)S(1)}, s32[128,9]{0,1:T(8,128)}, u32[]{:S(2)}) %copy-start.4) | copy-done | bytes 4632
  6.7 0.0 copy-start.7
  6.7 0.7 %copy-done.7 = s32[1,128]{1,0:T(1,128)S(1)} copy-done((s32[1,128]{1,0:T(1,128)S(1)}, s32[1,128]{1,0:T(1,128)}, u32[]{:S(2)}) %copy-start.7) | copy-done | bytes 536
  7.3 0.0 copy-start.8
  7.4 0.7 %copy-done.8 = s32[128]{0:T(128)S(1)} copy-done((s32[128]{0:T(128)S(1)}, s32[128]{0:T(128)}, u32[]{:S(2)}) %copy-start.8) | copy-done | bytes 536
  8.0 0.0 copy-start.5
  8.0 0.0 copy-start.6
  8.0 35.1 %shard_map.104 = (bf16[1024,256]{1,0:T(8,128)(2,1)S(1)}, bf16[2,2240,128]{2,1,0:T(8,128)(2,1)S(1)}, bf16[2,96,1024]{2,1,0:T(8,128)(2,1)S(1)}, bf16[8,256,640]{2,1,0:T(8,128)(2,1)S(1)}, s32[8,128]{1,0:T(8,128)S(1)}) custom-call(bf16[2048,1024]{1,0:T(8,128)(2,1)S(1)} %copy-done, bf16[2048,128]{1,0:T(8,128)(2,1)S(1)} %copy-done.2, f32[256,256]{1,0:T(8,128)S(1)} %copy-done.3, ...), custom_call_target="tpu_custom_call" | custom-call | flops 8000000000 | bytes 10485760 | tf_op jit(solution)/shard_map/pallas_call | solution.py:279
  43.1 0.0 copy-done.5
  43.1 0.0 copy-done.6
  43.1 17.4 %shard_map.105 = (bf16[2048,1024]{1,0:T(8,128)(2,1)}, f32[128,256]{1,0:T(8,128)S(1)}) custom-call(s32[8,128]{1,0:T(8,128)S(1)} %get-tuple-element.9.starts_ref, bf16[2048,1024]{1,0:T(8,128)(2,1)} %vin_ref.1, bf16[2,96,1024]{2,1,0:T(8,128)(2,1)S(1)} %get-tuple-element.10.halo_ref, bf16[2,2240,128]{2,1,0:T(8,128)(2,1)S(1)} %get-tuple-element.11.pan_ref, ...), custom_call_target="tpu_custom_call" | custom-call | flops 6000000000 | bytes 10485760 | tf_op jit(solution)/shard_map/pallas_call | solution.py:312
  60.5 2.3 %collective-permute-start = (f32[64,256]{1,0:T(8,128)S(1)}, f32[64,256]{1,0:T(8,128)S(1)}, u32[]{:S(2)}, u32[]{:S(2)}) collective-permute-start(f32[64,256]{1,0:T(8,128)S(1)} %constant_dynamic-slice_fusion), channel_id=1, source_target_pairs={{0,1},{1,0},{2,3},{3,2},{4,5},{5,4},{6,7},{7,6},{8,9},{9,8},{10,11... | collective-permute-start | bytes 196616 | tf_op jit(solution)/shard_map/ppermute | solution.py:351
  62.8 0.9 %collective-permute-done = f32[64,256]{1,0:T(8,128)S(1)} collective-permute-done((f32[64,256]{1,0:T(8,128)S(1)}, f32[64,256]{1,0:T(8,128)S(1)}, u32[]{:S(2)}, u32[]{:S(2)}) %collective-permute-start) | collective-permute-done | bytes 65568 | tf_op jit(solution)/shard_map/ppermute | solution.py:351
  63.7 0.6 dynamic-slice_add_fusion
  (1 shorter events, 0.0 us)
Async XLA Ops:
  0.6 2.2 %copy-start = (bf16[2048,1024]{1,0:T(8,128)(2,1)S(1)}, bf16[2048,1024]{1,0:T(8,128)(2,1)}, u32[]{:S(2)}) copy-start(bf16[2048,1024]{1,0:T(8,128)(2,1)} %vin_ref.1) | copy-start | bytes 12582916
  2.8 1.2 %copy-start.1 = (bf16[128,9,384]{2,0,1:T(8,128)(2,1)S(1)}, bf16[128,9,384]{2,0,1:T(8,128)(2,1)}, u32[]{:S(2)}) copy-start(bf16[128,9,384]{2,0,1:T(8,128)(2,1)} %param.14) | copy-start | bytes 2654212
  4.0 1.0 %copy-start.2 = (bf16[2048,128]{1,0:T(8,128)(2,1)S(1)}, bf16[2048,128]{1,0:T(8,128)(2,1)}, u32[]{:S(2)}) copy-start(bf16[2048,128]{1,0:T(8,128)(2,1)} %panel_ref.1) | copy-start | bytes 1572868
  5.0 0.9 %copy-start.3 = (f32[256,256]{1,0:T(8,128)S(1)}, f32[256,256]{1,0:T(8,128)}, u32[]{:S(2)}) copy-start(f32[256,256]{1,0:T(8,128)} %factor_ref.1) | copy-start | bytes 786436
  6.0 0.7 %copy-start.4 = (s32[128,9]{0,1:T(8,128)S(1)}, s32[128,9]{0,1:T(8,128)}, u32[]{:S(2)}) copy-start(s32[128,9]{0,1:T(8,128)} %param.15) | copy-start | bytes 13828
  6.7 0.7 %copy-start.7 = (s32[1,128]{1,0:T(1,128)S(1)}, s32[1,128]{1,0:T(1,128)}, u32[]{:S(2)}) copy-start(s32[1,128]{1,0:T(1,128)} %basis_ref.1) | copy-start | bytes 1540
  7.3 0.7 %copy-start.8 = (s32[128]{0:T(128)S(1)}, s32[128]{0:T(128)}, u32[]{:S(2)}) copy-start(s32[128]{0:T(128)} %param.13) | copy-start | bytes 1540
  8.0 35.1 %copy-start.5 = (s32[1024]{0:T(1024)S(1)}, s32[1024]{0:T(1024)}, u32[]{:S(2)}) copy-start(s32[1024]{0:T(1024)} %param.16) | copy-start | bytes 12292
  8.0 35.1 %copy-start.6 = (f32[1024]{0:T(1024)S(1)}, f32[1024]{0:T(1024)}, u32[]{:S(2)}) copy-start(f32[1024]{0:T(1024)} %param.17) | copy-start | bytes 12292
  60.5 3.2 %collective-permute-start = (f32[64,256]{1,0:T(8,128)S(1)}, f32[64,256]{1,0:T(8,128)S(1)}, u32[]{:S(2)}, u32[]{:S(2)}) collective-permute-start(f32[64,256]{1,0:T(8,128)S(1)} %constant_dynamic-slice_fusion), channel_id=1, source_target_pairs={{0,1},{1,0},{2,3},{3,2},{4,5},{5,4},{6,7},{7,6},{8,9},{9,8},{10,11... | collective-permute-start | bytes 196616 | tf_op jit(solution)/shard_map/ppermute | solution.py:351

commit v3 on v2

v3 whole, which is shorter than its diff:
```python
import functools

import jax
import jax.numpy as jnp
from jax import lax
from jax.experimental import pallas as pl
from jax.experimental.pallas import tpu as pltpu
from jax.sharding import PartitionSpec as P

NPMAX = 16
BMAX = 24
K = 9
RIM = (K - 1) // 2
HALO = RIM * BMAX
GROUP = 16
WIN = -(-(GROUP + K - 1) * BMAX // 128) * 128
FOLD = -(-K * BMAX // 128) * 128
F32 = jnp.float32
BF16 = jnp.bfloat16
MESH = pl.DeviceIdType.MESH


def iota(rows, columns, axis):
    return lax.broadcasted_iota(jnp.int32, (rows, columns), axis)


def group_of(rows, columns, axis, size, most):
    small = (8, columns) if axis == 1 else (rows, 128)
    index = iota(*small, axis)
    group = jnp.zeros(small, jnp.int32)
    for edge in range(1, most):
        group = group + jnp.where(index >= edge * size, 1, 0)
    return jnp.tile(group, (rows // small[0], columns // small[1]))


def mix_kernel(n, vec_hbm, panel_hbm, coupling_hbm, factor_ref, basis_ref, proj_ref, present_ref,
               mix_ref, pan_ref, base_ref, lean_ref,
               vec, part, got, counts, limit, spread, fold, cm_ref, halo_ref, band, first_ref, starts,
               ext, pext, padded, ppadded,
               load_sem, own_sem, cm_sem, start_sem, pan_sems, halo_sems, count_sems, inner_sems, mix_sems):
    row, col = lax.axis_index("row"), lax.axis_index("col")
    other = 1 - col
    up, down = lax.rem(row + 1, n), lax.rem(row + n - 1, n)
    rows, half = panel_hbm.shape
    slab = mix_ref.shape[0] // n
    body = pl.ds(HALO, rows)

    own = pltpu.make_async_copy(panel_hbm, pan_ref.at[col, body], own_sem)
    own.start()
    loads = pltpu.make_async_copy(vec_hbm, vec, load_sem)
    loads.start()
    blocks = pltpu.make_async_copy(coupling_hbm, cm_ref, cm_sem)
    blocks.start()

    barrier = pltpu.get_barrier_semaphore()
    for step in range(1, n):
        peer = lax.rem(row + step, n)
        pl.semaphore_signal(barrier, inc=1, device_id=(peer, col), device_id_type=MESH)
    for peer in (row, up, down):
        pl.semaphore_signal(barrier, inc=1, device_id=(peer, other), device_id_type=MESH)
    pl.semaphore_wait(barrier, n - 1 + 3)

    def remote(src, dst, sems, slot, target):
        return pltpu.make_async_remote_copy(
            src_ref=src, dst_ref=dst, send_sem=sems.at[(0,) + slot], recv_sem=sems.at[(1,) + slot],
            device_id=target, device_id_type=MESH)

    swap = remote(panel_hbm, pan_ref.at[col, pl.ds(HALO, rows)], pan_sems, (0,), (row, other))
    swap.start()
    count_copies = [
        remote(basis_ref, counts.at[side], count_sems, (side,), (target, col))
        for side, target in ((0, up), (1, down))
    ]
    for copy in count_copies:
        copy.start()
    halos = []
    for side, target in ((0, up), (1, down)):
        src_at = rows - HALO if side == 0 else 0
        dst_at = 0 if side == 0 else HALO + rows
        for where in (0, 1):
            to = col if where == 0 else other
            halos.append(remote(panel_hbm.at[pl.ds(src_at, HALO)], pan_ref.at[col, pl.ds(dst_at, HALO)],
                                pan_sems, (1 + 2 * side + where,), (target, to)))
        halos.append(remote(vec_hbm.at[pl.ds(src_at, HALO)], halo_ref.at[side], halo_sems, (side,), (target, col)))
    own.wait()
    loads.wait()

    def product(which, source):
        piece = lax.dot_general(source, vec[...], (((0,), (0,)), ((), ())), preferred_element_type=F32)
        part[which] = piece.T.astype(BF16)

    def inner_copy(which, step):
        peer = lax.rem(row + step, n)
        return remote(part.at[which, pl.ds(pl.multiple_of(peer * slab, slab), slab)],
                      got.at[which, step], inner_sems, (which, step), (peer, col))

    product(col, pan_ref[col, HALO:HALO + rows, :])
    for step in range(1, n):
        inner_copy(col, step).start()
    swap.wait_recv()
    product(other, pan_ref[other, HALO:HALO + rows, :])
    for step in range(1, n):
        inner_copy(other, step).start()
    for copy in halos:
        copy.start()

    atoms = cm_ref.shape[1]
    wide = cm_ref.shape[2]
    spread[...] = jnp.where(group_of(GROUP * NPMAX, wide, 1, BMAX, NPMAX) == (iota(GROUP * NPMAX, wide, 0) & 15),
                            1.0, 0.0)
    fold_slot = iota(wide, FOLD, 1) - BMAX * group_of(wide, FOLD, 1, BMAX, K)
    fold_from = iota(wide, FOLD, 0) - BMAX * group_of(wide, FOLD, 0, BMAX, NPMAX)
    fold[...] = jnp.where((fold_slot == fold_from) & (iota(wide, FOLD, 1) < K * BMAX), 1.0, 0.0).astype(BF16)
    for copy in count_copies:
        copy.wait_recv()
    blocks.wait()
    here = basis_ref[...].astype(F32)
    prev, post = counts[0].astype(F32), counts[1].astype(F32)
    lower = jnp.where(iota(atoms, atoms, 0) < iota(atoms, atoms, 1), 1.0, 0.0).astype(BF16)
    table = jnp.concatenate([prev, here, post, jnp.zeros((5, atoms), F32)], axis=0).astype(BF16)
    first = jnp.dot(table, lower, preferred_element_type=F32).astype(jnp.int32)
    first_ref[...] = jnp.clip(first + (HALO - rows) + rows * iota(8, atoms, 0), 0, rows + 2 * HALO)
    begin_copy = pltpu.make_async_copy(first_ref, starts, start_sem)
    begin_copy.start()
    lines = []
    at = iota(1, atoms, 1)
    for k in range(K):
        d = k - RIM
        near = here
        if d != 0:
            turn = (-d) % atoms
            inside = (at + d >= 0) & (at + d < atoms)
            near = jnp.where(inside, pltpu.roll(here, turn, 1), pltpu.roll(prev if d < 0 else post, turn, 1))
        lines.append(jnp.where(present_ref[k:k + 1, :] > 0, near, 0.0))
    lines.append(proj_ref[...].astype(F32))
    lines.append(jnp.zeros((atoms - K - 1, atoms), F32))
    limit[...] = jnp.concatenate(lines, axis=0).T

    lane = iota(GROUP, FOLD, 1)
    in_k = group_of(GROUP, FOLD, 1, BMAX, K)
    slot = (lane - BMAX * in_k).astype(F32)

    def band_step(t, carry):
        chunk = pl.ds(pl.multiple_of(t * GROUP, GROUP), GROUP)
        bounds = limit[chunk, :]
        reach = jnp.zeros((GROUP, FOLD), F32)
        for k in range(K):
            reach = jnp.where(in_k == k, bounds[:, k:k + 1], reach)
        kept = jnp.where(slot < reach, 1.0, 0.0)
        kept = jnp.broadcast_to(kept[:, None, :], (GROUP, NPMAX, FOLD)).reshape(GROUP * NPMAX, FOLD)
        most = jnp.broadcast_to(bounds[:, K:K + 1], (GROUP, FOLD))
        most = jnp.broadcast_to(most[:, None, :], (GROUP, NPMAX, FOLD)).reshape(GROUP * NPMAX, FOLD)
        valid = (kept > 0.5) & ((iota(GROUP * NPMAX, FOLD, 0) & 15).astype(F32) < most)
        which_k = group_of(GROUP * NPMAX, FOLD, 1, BMAX, K)
        acc = jnp.zeros((GROUP * NPMAX, FOLD), F32)
        for k in range(K):
            block = cm_ref[k, chunk, :].astype(F32)
            block = jnp.broadcast_to(block[:, None, :], (GROUP, NPMAX, wide)).reshape(GROUP * NPMAX, wide)
            folded = jnp.dot((block * spread[...]).astype(BF16), fold[...], preferred_element_type=F32)
            acc = jnp.where(which_k == k, folded, acc)
        acc = jnp.where(valid, acc, 0.0)
        acc = jnp.concatenate([acc, jnp.zeros((acc.shape[0], WIN - FOLD), F32)], axis=1)
        pieces = []
        for a in range(GROUP):
            piece = acc[a * NPMAX:(a + 1) * NPMAX]
            pieces.append(piece if a == 0 else pltpu.roll(piece, a * BMAX, 1))
        band[t] = jnp.concatenate(pieces, axis=0).astype(BF16)
        return carry

    lax.fori_loop(0, atoms // GROUP, band_step, 0)

    begin_copy.wait()
    for copy in halos:
        copy.wait()
    length = ext.shape[1]
    lanes = [slice(c * 128, (c + 1) * 128) for c in range(ext.shape[0])]
    chunk_rows = rows // 8

    def widen(t, carry):
        at = pl.multiple_of(t * chunk_rows, 16)
        block = vec[pl.ds(at, chunk_rows), :].astype(F32)
        for c, span in enumerate(lanes):
            ext[c, pl.ds(HALO + at, chunk_rows), :] = block[:, span]
        return carry

    lax.fori_loop(0, 8, widen, 0)
    for side, at in ((0, 0), (1, HALO + rows)):
        block = halo_ref[side].astype(F32)
        for c, span in enumerate(lanes):
            ext[c, at:at + HALO, :] = block[:, span]
    spare = length - 2 * HALO - rows
    ext[:, length - spare:, :] = jnp.zeros((ext.shape[0], spare, 128), F32)
    for which in (0, 1):
        pext[which, 0:length - spare, :] = pan_ref[which].astype(F32)
    pext[:, length - spare:, :] = jnp.zeros((2, spare, half), F32)
    used = (atoms + 2 * RIM) * BMAX
    padded[used:, :] = jnp.zeros((padded.shape[0] - used, padded.shape[1]), BF16)
    ppadded[used:, :] = jnp.zeros((ppadded.shape[0] - used, ppadded.shape[1]), BF16)

    def gather(t, carry):
        at = pl.multiple_of(2 * t * BMAX, 16)
        begins = []
        for e in (0, 1):
            flat = 2 * t + e + atoms - RIM
            begins.append(starts[lax.div(flat, atoms), lax.rem(flat, atoms)])
        for c, span in enumerate(lanes):
            both = [ext[c, pl.ds(begin, BMAX), :] for begin in begins]
            padded[pl.ds(at, 2 * BMAX), span] = jnp.concatenate(both, axis=0).astype(BF16)
        for c in (0, 1):
            both = [pext[c, pl.ds(begin, BMAX), :] for begin in begins]
            ppadded[pl.ds(at, 2 * BMAX), c * half:(c + 1) * half] = jnp.concatenate(both, axis=0).astype(BF16)
        return carry

    lax.fori_loop(0, (atoms + 2 * RIM) // 2, gather, 0)

    mine = pl.ds(pl.multiple_of(row * slab, slab), slab)
    sums = []
    for which in (0, 1):
        sums.append(part[which, mine, :].astype(F32))
    for step in range(1, n):
        for which in (0, 1):
            inner_copy(which, step).wait_recv()
            sums[which] = sums[which] + got[which, step].astype(F32)
    inner = jnp.concatenate(sums, axis=1)
    mixed = jnp.dot(inner, factor_ref[...], precision=lax.Precision.HIGHEST, preferred_element_type=F32)
    mix_ref[mine, :] = mixed.astype(BF16)

    def mix_copy(step):
        peer = lax.rem(row + step, n)
        return remote(mix_ref.at[mine], mix_ref.at[mine], mix_sems, (step,), (peer, col))

    for step in range(1, n):
        mix_copy(step).start()

    def project(g, carry):
        at = pl.ds(pl.multiple_of(g * GROUP * BMAX, 16), WIN)
        base_ref[g] = jnp.dot(band[g], padded[at, :], preferred_element_type=F32)
        lean_ref[g] = jnp.dot(band[g], ppadded[at, :], preferred_element_type=F32).astype(BF16)
        return carry

    lax.fori_loop(0, atoms // GROUP, project, 0)
    swap.wait_send()
    for copy in count_copies:
        copy.wait_send()
    for step in range(1, n):
        for which in (0, 1):
            inner_copy(which, step).wait_send()
    for step in range(1, n):
        mix_copy(step).wait()


def density_kernel(vin_ref, pan_ref, mix_ref, base_ref, lean_ref, mask_ref, occ_ref,
                   vec_ref, den_ref, mixing, weight, *, column_total):
    step = pl.program_id(0)
    tile = vin_ref.shape[0]

    @pl.when(step == 0)
    def _():
        mixing[...] = mix_ref[...].T
        weight[...] = mask_ref[...].astype(F32) * occ_ref[...] / column_total

    at = pl.ds(pl.multiple_of(HALO + step * tile, 16), tile)
    panel = jnp.concatenate([pan_ref[0, at, :], pan_ref[1, at, :]], axis=1)
    update = jnp.dot(panel, mixing[...], preferred_element_type=F32)
    vec_ref[...] = (vin_ref[...].astype(F32) - update).astype(BF16)
    update = jnp.dot(lean_ref[step], mixing[...], preferred_element_type=F32)
    rounded = (base_ref[step] - update).astype(BF16)
    weighted = (rounded.astype(F32) * weight[...]).astype(BF16)
    full = lax.dot_general(weighted, rounded, (((1,), (1,)), ((), ())), preferred_element_type=F32)
    shape = full.shape
    full = jnp.where(iota(*shape, 0) >> 4 == iota(*shape, 1) >> 4, full, 0.0)
    expand = jnp.where((iota(shape[1], NPMAX * NPMAX, 0) & 15) == (iota(shape[1], NPMAX * NPMAX, 1) & 15),
                       1.0, 0.0).astype(BF16)
    spreads = 0.0
    for _ in range(3):
        top = full.astype(BF16)
        spreads = spreads + jnp.dot(top, expand, preferred_element_type=F32)
        full = full - top.astype(F32)
    shape = spreads.shape
    spreads = jnp.where((iota(*shape, 0) & 15) == iota(*shape, 1) >> 4, spreads, 0.0)
    den_ref[...] = spreads.reshape(GROUP, NPMAX, shape[1]).sum(axis=1)


def local(vectors_in, panel, factor, atom_basis, proj_count, coupling, block_present, occ_mask, occ_weight):
    n = lax.axis_size("row")
    rows, cols = vectors_in.shape
    half = panel.shape[1]
    npan = factor.shape[0]
    atoms = atom_basis.shape[1]
    groups = atoms // GROUP
    vmem = pl.BlockSpec(memory_space=pltpu.VMEM)
    hbm = pl.BlockSpec(memory_space=pl.ANY)
    slab = cols // n
    ext_rows = rows + 2 * HALO
    pad_rows = (groups - 1) * GROUP * BMAX + WIN
    dma = pltpu.SemaphoreType.DMA
    operands = (vectors_in, panel, jnp.swapaxes(coupling, 0, 1), factor, atom_basis, proj_count[None, :], block_present.T)
    operands = [pltpu.with_memory_space_constraint(x, pltpu.HBM) for x in operands]
    mix, pan, base, lean = pl.pallas_call(
        functools.partial(mix_kernel, n),
        out_shape=(
            jax.ShapeDtypeStruct((cols, npan), BF16),
            jax.ShapeDtypeStruct((2, ext_rows, half), BF16),
            jax.ShapeDtypeStruct((groups, GROUP * NPMAX, cols), F32),
            jax.ShapeDtypeStruct((groups, GROUP * NPMAX, npan), BF16),
        ),
        in_specs=[hbm] * 3 + [vmem] * 4,
        out_specs=(vmem,) * 4,
        scratch_shapes=[
            pltpu.VMEM((rows, cols), BF16),
            pltpu.VMEM((2, cols, half), BF16),
            pltpu.VMEM((2, n, slab, half), BF16),
            pltpu.VMEM((2, 1, atoms), jnp.int32),
            pltpu.VMEM((atoms, atoms), F32),
            pltpu.VMEM((GROUP * NPMAX, NPMAX * BMAX), F32),
            pltpu.VMEM((NPMAX * BMAX, FOLD), BF16),
            pltpu.VMEM((K, atoms, NPMAX * BMAX), BF16),
            pltpu.VMEM((2, HALO, cols), BF16),
            pltpu.VMEM((groups, GROUP * NPMAX, WIN), BF16),
            pltpu.VMEM((8, atoms), jnp.int32),
            pltpu.SMEM((8, atoms), jnp.int32),
            pltpu.VMEM((cols // 128, ext_rows + BMAX, 128), F32),
            pltpu.VMEM((2, ext_rows + BMAX, half), F32),
            pltpu.VMEM((pad_rows, cols), BF16),
            pltpu.VMEM((pad_rows, npan), BF16),
            dma, dma, dma, dma, dma((2, 5)), dma((2, 2)), dma((2, 2)), dma((2, 2, n)), dma((2, n)),
        ],
        compiler_params=pltpu.CompilerParams(collective_id=0, has_side_effects=True, vmem_limit_bytes=40 << 20),
        cost_estimate=pl.CostEstimate(flops=8 * 10**9, bytes_accessed=10 << 20, transcendentals=0),
    )(*operands)

    tile = rows // groups
    vectors, partial = pl.pallas_call(
        functools.partial(density_kernel, column_total=cols * lax.axis_size("col")),
        out_shape=(
            jax.ShapeDtypeStruct((rows, cols), BF16),
            jax.ShapeDtypeStruct((atoms, NPMAX * NPMAX), F32),
        ),
        grid=(groups,),
        in_specs=[pl.BlockSpec((tile, cols), lambda s: (s, 0))] + [vmem] * 6,
        out_specs=[
            pl.BlockSpec((tile, cols), lambda s: (s, 0)),
            pl.BlockSpec((GROUP, NPMAX * NPMAX), lambda s: (s, 0)),
        ],
        scratch_shapes=[pltpu.VMEM((npan, cols), BF16), pltpu.VMEM((1, cols), F32)],
        compiler_params=pltpu.CompilerParams(vmem_limit_bytes=16 << 20),
        cost_estimate=pl.CostEstimate(flops=6 * 10**9, bytes_accessed=10 << 20, transcendentals=0),
    )(operands[0], pan, mix, base, lean, occ_mask[None, :], occ_weight[None, :])

    ncol = lax.axis_size("col")
    share = atoms // ncol
    col = lax.axis_index("col")
    density = lax.dynamic_slice_in_dim(partial, col * share, share, 0)
    for step in range(1, ncol):
        sent = lax.dynamic_slice_in_dim(partial, lax.rem(col + step, ncol) * share, share, 0)
        density = density + lax.ppermute(sent, "col", [(i, (i + step) % ncol) for i in range(ncol)])
    return (vectors, density)


def solution(mesh):
    placed = (
        P("row", "col"),
        P("row", "col"),
        P(),
        P("row", None),
        P("row"),
        P("row", None, None),
        P("row", None),
        P("col"),
        P("col"),
    )
    return jax.shard_map(
        local,
        mesh=mesh,
        in_specs=placed,
        out_specs=(P("row", "col"), P(("row", "col"), None)),
        check_vma=False,
    )
```

time: 64.7 us -> 54.9 us (0.85)
  the two profiles are of different devices: /device:TPU:27 before, /device:TPU:15 now
where the time goes in v3:
time: 54.9 us; the launch traced here: 54.6 us
  Pallas kernels  51.5 us (94%)
  waiting for transfers between devices  0.9 us (2%)
  starting transfers between devices  0.79 us (1%)
  between operations  0.69 us (1%)
  other arithmetic  0.64 us (1%)
    pallas_call x1, Pallas kernels, local(): pl.pallas_call(functools.partial(mix_kernel, n), out_shape=(jax.ShapeDtyp...  41.9 us
    pallas_call x1, Pallas kernels, local(): pl.pallas_call(functools.partial(density_kernel, column_total=cols * lax....  9.68 us
  transfers between devices with their start and end apart: 1, of which 1 were waited for; matrix products, arithmetic and copies ran while one was open for 0% of the time, Pallas kernels for 0%

profile of v3, /device:TPU:15, one launch (start us, length us, event | category | flops | bytes accessed | tf_op | source)
XLA Modules:
  0.0 54.6 jit_solution(1392962380071796266)
XLA Ops:
  0.6 0.0 copy-start
  0.7 0.0 copy-start.1
  0.7 41.9 %shard_map.104 = (bf16[1024,256]{1,0:T(8,128)(2,1)S(1)}, bf16[2,2240,128]{2,1,0:T(8,128)(2,1)S(1)}, f32[8,256,1024]{2,1,0:T(8,128)S(1)}, bf16[8,256,256]{2,1,0:T(8,128)(2,1)S(1)}) custom-call(bf16[2048,1024]{1,0:T(8,128)(2,1)} %vin_ref.1, bf16[2048,128]{1,0:T(8,128)(2,1)} %panel_hbm.1, bf16[9,128,384]{2,1,0:T(8,128)(2,1)} %bitcast.7, f32[256,256]{1,0:T(8,128)} %factor_ref.1, ...), custom_call_target="tpu_custom_call" | custom-call | flops 8000000000 | bytes 10485760 | tf_op jit(solution)/shard_map/pallas_call | solution.py:299
  42.5 0.0 copy-done
  42.5 0.0 copy-done.1
  42.6 9.7 %shard_map.105 = (bf16[2048,1024]{1,0:T(8,128)(2,1)}, f32[128,256]{1,0:T(8,128)S(1)}) custom-call(bf16[2048,1024]{1,0:T(8,128)(2,1)} %vin_ref.1, bf16[2,2240,128]{2,1,0:T(8,128)(2,1)S(1)} %get-tuple-element.8.pan_ref, bf16[1024,256]{1,0:T(8,128)(2,1)S(1)} %get-tuple-element.9.mix_ref, f32[8,256,1024]{2,1,0:T(8,128)S(1)} %get-tuple-element.10.base_ref, ...), custom_call_target="tpu_custom_call" | custom-call | flops 6000000000 | bytes 10485760 | tf_op jit(solution)/shard_map/pallas_call | solution.py:333
  52.2 0.8 %collective-permute-start = (f32[64,256]{1,0:T(8,128)S(1)}, f32[64,256]{1,0:T(8,128)S(1)}, u32[]{:S(2)}, u32[]{:S(2)}) collective-permute-start(f32[64,256]{1,0:T(8,128)S(1)} %constant_dynamic-slice_fusion), channel_id=1, source_target_pairs={{0,1},{1,0},{2,3},{3,2},{4,5},{5,4},{6,7},{7,6},{8,9},{9,8},{10,11... | collective-permute-start | bytes 196616 | tf_op jit(solution)/shard_map/ppermute | solution.py:356
  53.0 0.9 %collective-permute-done = f32[64,256]{1,0:T(8,128)S(1)} collective-permute-done((f32[64,256]{1,0:T(8,128)S(1)}, f32[64,256]{1,0:T(8,128)S(1)}, u32[]{:S(2)}, u32[]{:S(2)}) %collective-permute-start) | collective-permute-done | bytes 65568 | tf_op jit(solution)/shard_map/ppermute | solution.py:356
  53.9 0.6 %dynamic-slice_add_fusion = f32[64,256]{1,0:T(8,128)} fusion(f32[64,256]{1,0:T(8,128)S(1)} %collective-permute-done, f32[128,256]{1,0:T(8,128)S(1)} %get-tuple-element.13, s32[]{:T(128)S(6)} %select_n.6), kind=kLoop, calls=%fused_computation | loop fusion | flops 16384 | bytes 196612 | tf_op jit(solution)/shard_map/add | solution.py:356
  (1 shorter events, 0.0 us)
Async XLA Ops:
  0.6 41.9 %copy-start = (s32[1024]{0:T(1024)S(1)}, s32[1024]{0:T(1024)}, u32[]{:S(2)}) copy-start(s32[1024]{0:T(1024)} %param.16) | copy-start | bytes 12292
  0.7 41.9 %copy-start.1 = (f32[1024]{0:T(1024)S(1)}, f32[1024]{0:T(1024)}, u32[]{:S(2)}) copy-start(f32[1024]{0:T(1024)} %param.17) | copy-start | bytes 12292
  52.2 1.7 %collective-permute-start = (f32[64,256]{1,0:T(8,128)S(1)}, f32[64,256]{1,0:T(8,128)S(1)}, u32[]{:S(2)}, u32[]{:S(2)}) collective-permute-start(f32[64,256]{1,0:T(8,128)S(1)} %constant_dynamic-slice_fusion), channel_id=1, source_target_pairs={{0,1},{1,0},{2,3},{3,2},{4,5},{5,4},{6,7},{7,6},{8,9},{9,8},{10,11... | collective-permute-start | bytes 196616 | tf_op jit(solution)/shard_map/ppermute | solution.py:356

commit v4 on v3

--- a/solution.py
+++ b/solution.py
@@ -33,17 +33,26 @@
     return jnp.tile(group, (rows // small[0], columns // small[1]))
 
 
-def mix_kernel(n, vec_hbm, panel_hbm, coupling_hbm, factor_ref, basis_ref, proj_ref, present_ref,
+def mix_kernel(n, plane, vec_hbm, panel_hbm, coupling_hbm, factor_ref, basis_ref, proj_ref, present_ref,
                mix_ref, pan_ref, base_ref, lean_ref,
-               vec, part, got, counts, limit, spread, fold, cm_ref, halo_ref, band, first_ref, starts,
+               vec, part, got, middle, got_line, counts, limit, spread, fold, cm_ref, halo_ref, band, first_ref, starts,
                ext, pext, padded, ppadded,
-               load_sem, own_sem, cm_sem, start_sem, pan_sems, halo_sems, count_sems, inner_sems, mix_sems):
+               load_sem, own_sem, cm_sem, start_sem, pan_sems, halo_sems, count_sems, plane_sems, line_sems, mix_sems, pass_sems):
     row, col = lax.axis_index("row"), lax.axis_index("col")
     other = 1 - col
     up, down = lax.rem(row + 1, n), lax.rem(row + n - 1, n)
     rows, half = panel_hbm.shape
     slab = mix_ref.shape[0] // n
     body = pl.ds(HALO, rows)
+    q, p = n // plane, plane
+    line, spot = lax.div(row, p), lax.rem(row, p)
+
+    def plane_peer(step):
+        return line * p + lax.rem(spot + step, p)
+
+    def line_peer(step):
+        return lax.rem(line + step, q) * p + spot
+
 
     own = pltpu.make_async_copy(panel_hbm, pan_ref.at[col, body], own_sem)
     own.start()
@@ -53,12 +62,11 @@
     blocks.start()
 
     barrier = pltpu.get_barrier_semaphore()
-    for step in range(1, n):
-        peer = lax.rem(row + step, n)
-        pl.semaphore_signal(barrier, inc=1, device_id=(peer, col), device_id_type=MESH)
-    for peer in (row, up, down):
-        pl.semaphore_signal(barrier, inc=1, device_id=(peer, other), device_id_type=MESH)
-    pl.semaphore_wait(barrier, n - 1 + 3)
+    greeted = [(plane_peer(step), col) for step in range(1, p)] + [(line_peer(step), col) for step in range(1, q)]
+    greeted += [(up, col), (down, col)] + [(peer, other) for peer in (row, up, down)]
+    for target in greeted:
+        pl.semaphore_signal(barrier, inc=1, device_id=target, device_id_type=MESH)
+    pl.semaphore_wait(barrier, len(greeted))
 
     def remote(src, dst, sems, slot, target):
         return pltpu.make_async_remote_copy(
@@ -87,20 +95,27 @@
 
     def product(which, source):
         piece = lax.dot_general(source, vec[...], (((0,), (0,)), ((), ())), preferred_element_type=F32)
-        part[which] = piece.T.astype(BF16)
-
-    def inner_copy(which, step):
-        peer = lax.rem(row + step, n)
-        return remote(part.at[which, pl.ds(pl.multiple_of(peer * slab, slab), slab)],
-                      got.at[which, step], inner_sems, (which, step), (peer, col))
+        piece = piece.T.astype(BF16)
+        for z in range(q):
+            for at in range(p):
+                part[which, at, z * slab:(z + 1) * slab] = piece[(z * p + at) * slab:(z * p + at + 1) * slab]
+
+    def plane_copy(which, step):
+        return remote(part.at[which, lax.rem(spot + step, p)], got.at[which, step], plane_sems, (which, step),
+                      (plane_peer(step), col))
+
+    def line_copy(which, step):
+        at = pl.multiple_of(lax.rem(line + step, q) * slab, slab)
+        return remote(middle.at[which, pl.ds(at, slab)], got_line.at[which, step], line_sems, (which, step),
+                      (line_peer(step), col))
 
     product(col, pan_ref[col, HALO:HALO + rows, :])
-    for step in range(1, n):
-        inner_copy(col, step).start()
+    for step in range(1, p):
+        plane_copy(col, step).start()
     swap.wait_recv()
     product(other, pan_ref[other, HALO:HALO + rows, :])
-    for step in range(1, n):
-        inner_copy(other, step).start()
+    for step in range(1, p):
+        plane_copy(other, step).start()
     for copy in halos:
         copy.start()
 
@@ -169,6 +184,15 @@
 
     lax.fori_loop(0, atoms // GROUP, band_step, 0)
 
+    for which in (0, 1):
+        total = part[which, spot].astype(F32)
+        for step in range(1, p):
+            plane_copy(which, step).wait_recv()
+            total = total + got[which, step].astype(F32)
+        middle[which] = total.astype(BF16)
+        for step in range(1, q):
+            line_copy(which, step).start()
+
     begin_copy.wait()
     for copy in halos:
         copy.wait()
@@ -197,6 +221,31 @@
     padded[used:, :] = jnp.zeros((padded.shape[0] - used, padded.shape[1]), BF16)
     ppadded[used:, :] = jnp.zeros((ppadded.shape[0] - used, ppadded.shape[1]), BF16)
 
+    mine = pl.ds(pl.multiple_of(row * slab, slab), slab)
+    sums = []
+    for which in (0, 1):
+        total = middle[which, pl.ds(pl.multiple_of(line * slab, slab), slab), :].astype(F32)
+        for step in range(1, q):
+            line_copy(which, step).wait_recv()
+            total = total + got_line[which, step].astype(F32)
+        sums.append(total)
+    inner = jnp.concatenate(sums, axis=1)
+    mixed = jnp.dot(inner, factor_ref[...], precision=lax.Precision.HIGHEST, preferred_element_type=F32)
+    mix_ref[mine, :] = mixed.astype(BF16)
+
+    def mix_copy(step):
+        return remote(mix_ref.at[mine], mix_ref.at[mine], mix_sems, (step,), (line_peer(step), col))
+
+    def pass_copy(z, step):
+        at = pl.multiple_of((lax.rem(line + q - z, q) * p + spot) * slab, slab)
+        return remote(mix_ref.at[pl.ds(at, slab)], mix_ref.at[pl.ds(at, slab)], pass_sems, (z, step),
+                      (plane_peer(step), col))
+
+    for step in range(1, q):
+        mix_copy(step).start()
+    for step in range(1, p):
+        pass_copy(0, step).start()
+
     def gather(t, carry):
         at = pl.multiple_of(2 * t * BMAX, 16)
         begins = []
@@ -213,24 +262,10 @@
 
     lax.fori_loop(0, (atoms + 2 * RIM) // 2, gather, 0)
 
-    mine = pl.ds(pl.multiple_of(row * slab, slab), slab)
-    sums = []
-    for which in (0, 1):
-        sums.append(part[which, mine, :].astype(F32))
-    for step in range(1, n):
-        for which in (0, 1):
-            inner_copy(which, step).wait_recv()
-            sums[which] = sums[which] + got[which, step].astype(F32)
-    inner = jnp.concatenate(sums, axis=1)
-    mixed = jnp.dot(inner, factor_ref[...], precision=lax.Precision.HIGHEST, preferred_element_type=F32)
-    mix_ref[mine, :] = mixed.astype(BF16)
-
-    def mix_copy(step):
-        peer = lax.rem(row + step, n)
-        return remote(mix_ref.at[mine], mix_ref.at[mine], mix_sems, (step,), (peer, col))
-
-    for step in range(1, n):
-        mix_copy(step).start()
+    for z in range(1, q):
+        mix_copy(z).wait_recv()
+        for step in range(1, p):
+            pass_copy(z, step).start()
 
     def project(g, carry):
         at = pl.ds(pl.multiple_of(g * GROUP * BMAX, 16), WIN)
@@ -242,11 +277,16 @@
     swap.wait_send()
     for copy in count_copies:
         copy.wait_send()
-    for step in range(1, n):
-        for which in (0, 1):
-            inner_copy(which, step).wait_send()
-    for step in range(1, n):
-        mix_copy(step).wait()
+    for which in (0, 1):
+        for step in range(1, p):
+            plane_copy(which, step).wait_send()
+        for step in range(1, q):
+            line_copy(which, step).wait_send()
+    for step in range(1, q):
+        mix_copy(step).wait_send()
+    for z in range(q):
+        for step in range(1, p):
+            pass_copy(z, step).wait()
 
 
 def density_kernel(vin_ref, pan_ref, mix_ref, base_ref, lean_ref, mask_ref, occ_ref,
@@ -291,13 +331,14 @@
     vmem = pl.BlockSpec(memory_space=pltpu.VMEM)
     hbm = pl.BlockSpec(memory_space=pl.ANY)
     slab = cols // n
+    plane = max(d for d in range(1, n + 1) if n % d == 0 and d * d <= n)
     ext_rows = rows + 2 * HALO
     pad_rows = (groups - 1) * GROUP * BMAX + WIN
     dma = pltpu.SemaphoreType.DMA
     operands = (vectors_in, panel, jnp.swapaxes(coupling, 0, 1), factor, atom_basis, proj_count[None, :], block_present.T)
     operands = [pltpu.with_memory_space_constraint(x, pltpu.HBM) for x in operands]
     mix, pan, base, lean = pl.pallas_call(
-        functools.partial(mix_kernel, n),
+        functools.partial(mix_kernel, n, plane),
         out_shape=(
             jax.ShapeDtypeStruct((cols, npan), BF16),
             jax.ShapeDtypeStruct((2, ext_rows, half), BF16),
@@ -308,8 +349,10 @@
         out_specs=(vmem,) * 4,
         scratch_shapes=[
             pltpu.VMEM((rows, cols), BF16),
-            pltpu.VMEM((2, cols, half), BF16),
-            pltpu.VMEM((2, n, slab, half), BF16),
+            pltpu.VMEM((2, plane, cols // plane, half), BF16),
+            pltpu.VMEM((2, plane, cols // plane, half), BF16),
+            pltpu.VMEM((2, cols // plane, half), BF16),
+            pltpu.VMEM((2, n // plane, slab, half), BF16),
             pltpu.VMEM((2, 1, atoms), jnp.int32),
             pltpu.VMEM((atoms, atoms), F32),
             pltpu.VMEM((GROUP * NPMAX, NPMAX * BMAX), F32),
@@ -323,7 +366,8 @@
             pltpu.VMEM((2, ext_rows + BMAX, half), F32),
             pltpu.VMEM((pad_rows, cols), BF16),
             pltpu.VMEM((pad_rows, npan), BF16),
-            dma, dma, dma, dma, dma((2, 5)), dma((2, 2)), dma((2, 2)), dma((2, 2, n)), dma((2, n)),
+            dma, dma, dma, dma, dma((2, 5)), dma((2, 2)), dma((2, 2)),
+            dma((2, 2, plane)), dma((2, 2, n // plane)), dma((2, n // plane)), dma((2, n // plane, plane)),
         ],
         compiler_params=pltpu.CompilerParams(collective_id=0, has_side_effects=True, vmem_limit_bytes=40 << 20),
         cost_estimate=pl.CostEstimate(flops=8 * 10**9, bytes_accessed=10 << 20, transcendentals=0),

time: 54.9 us -> 49.9 us (0.909)
  the two profiles are of different devices: /device:TPU:15 before, /device:TPU:0 now
where the time goes in v4:
time: 49.9 us; the launch traced here: 49.6 us
  Pallas kernels  47 us (94%)
  waiting for transfers between devices  1.24 us (2%)
  between operations  0.7 us (1%)
  other arithmetic  0.64 us (1%)
    pallas_call x1, Pallas kernels, local(): pl.pallas_call(functools.partial(mix_kernel, n, plane), out_shape=(jax.Sh...  37.3 us
    pallas_call x1, Pallas kernels, local(): pl.pallas_call(functools.partial(density_kernel, column_total=cols * lax....  9.67 us
    ppermute x1, waiting for transfers between devices, local(): lax.ppermute(sent, 'col', [(i, (i + step) % ncol) for i in range(ncol)])  1.24 us
  transfers between devices with their start and end apart: 1, of which 1 were waited for; matrix products, arithmetic and copies ran while one was open for 0% of the time, Pallas kernels for 0%

profile of v4, /device:TPU:0, one launch (start us, length us, event | category | flops | bytes accessed | tf_op | source)
XLA Modules:
  0.0 49.6 jit_solution(1338376578499536599)
XLA Ops:
  0.6 0.0 copy-start
  0.7 0.0 copy-start.1
  0.7 37.3 %shard_map.104 = (bf16[1024,256]{1,0:T(8,128)(2,1)S(1)}, bf16[2,2240,128]{2,1,0:T(8,128)(2,1)S(1)}, f32[8,256,1024]{2,1,0:T(8,128)S(1)}, bf16[8,256,256]{2,1,0:T(8,128)(2,1)S(1)}) custom-call(bf16[2048,1024]{1,0:T(8,128)(2,1)} %vin_ref.1, bf16[2048,128]{1,0:T(8,128)(2,1)} %panel_hbm.1, bf16[9,128,384]{2,1,0:T(8,128)(2,1)} %bitcast.7, f32[256,256]{1,0:T(8,128)} %factor_ref.1, ...), custom_call_target="tpu_custom_call" | custom-call | flops 8000000000 | bytes 10485760 | tf_op jit(solution)/shard_map/pallas_call | solution.py:340
  38.0 0.0 copy-done
  38.0 0.0 copy-done.1
  38.0 9.7 %shard_map.105 = (bf16[2048,1024]{1,0:T(8,128)(2,1)}, f32[128,256]{1,0:T(8,128)S(1)}) custom-call(bf16[2048,1024]{1,0:T(8,128)(2,1)} %vin_ref.1, bf16[2,2240,128]{2,1,0:T(8,128)(2,1)S(1)} %get-tuple-element.8.pan_ref, bf16[1024,256]{1,0:T(8,128)(2,1)S(1)} %get-tuple-element.9.mix_ref, f32[8,256,1024]{2,1,0:T(8,128)S(1)} %get-tuple-element.10.base_ref, ...), custom_call_target="tpu_custom_call" | custom-call | flops 6000000000 | bytes 10485760 | tf_op jit(solution)/shard_map/pallas_call | solution.py:377
  47.7 0.0 collective-permute-start
  47.7 1.2 %collective-permute-done = f32[64,256]{1,0:T(8,128)S(1)} collective-permute-done((f32[64,256]{1,0:T(8,128)S(1)}, f32[64,256]{1,0:T(8,128)S(1)}, u32[]{:S(2)}, u32[]{:S(2)}) %collective-permute-start) | collective-permute-done | bytes 65568 | tf_op jit(solution)/shard_map/ppermute | solution.py:400
  48.9 0.6 %dynamic-slice_add_fusion = f32[64,256]{1,0:T(8,128)} fusion(f32[64,256]{1,0:T(8,128)S(1)} %collective-permute-done, f32[128,256]{1,0:T(8,128)S(1)} %get-tuple-element.13, s32[]{:T(128)S(6)} %select_n.6), kind=kLoop, calls=%fused_computation | loop fusion | flops 16384 | bytes 196612 | tf_op jit(solution)/shard_map/add | solution.py:400
  (1 shorter events, 0.0 us)
Async XLA Ops:
  0.6 37.3 %copy-start = (s32[1024]{0:T(1024)S(1)}, s32[1024]{0:T(1024)}, u32[]{:S(2)}) copy-start(s32[1024]{0:T(1024)} %param.16) | copy-start | bytes 12292
  0.7 37.3 %copy-start.1 = (f32[1024]{0:T(1024)S(1)}, f32[1024]{0:T(1024)}, u32[]{:S(2)}) copy-start(f32[1024]{0:T(1024)} %param.17) | copy-start | bytes 12292
  47.7 1.3 %collective-permute-start = (f32[64,256]{1,0:T(8,128)S(1)}, f32[64,256]{1,0:T(8,128)S(1)}, u32[]{:S(2)}, u32[]{:S(2)}) collective-permute-start(f32[64,256]{1,0:T(8,128)S(1)} %constant_dynamic-slice_fusion), channel_id=1, source_target_pairs={{0,1},{1,0},{2,3},{3,2},{4,5},{5,4},{6,7},{7,6},{8,9},{9,8},{10,11... | collective-permute-start | bytes 196616 | tf_op jit(solution)/shard_map/ppermute | solution.py:400

commit v5 on v4

--- a/solution.py
+++ b/solution.py
@@ -56,8 +56,12 @@
 
     own = pltpu.make_async_copy(panel_hbm, pan_ref.at[col, body], own_sem)
     own.start()
-    loads = pltpu.make_async_copy(vec_hbm, vec, load_sem)
-    loads.start()
+    early = pl.ds(0, rows // 2)
+    late = pl.ds(rows // 2, rows // 2)
+    loads = [pltpu.make_async_copy(vec_hbm.at[part_rows], vec.at[part_rows], load_sem.at[i])
+             for i, part_rows in enumerate((early, late))]
+    for load in loads:
+        load.start()
     blocks = pltpu.make_async_copy(coupling_hbm, cm_ref, cm_sem)
     blocks.start()
 
@@ -66,6 +70,16 @@
     greeted += [(up, col), (down, col)] + [(peer, other) for peer in (row, up, down)]
     for target in greeted:
         pl.semaphore_signal(barrier, inc=1, device_id=target, device_id_type=MESH)
+    atoms, wide = cm_ref.shape[1:]
+    spread[...] = jnp.where(group_of(GROUP * NPMAX, wide, 1, BMAX, NPMAX) == (iota(GROUP * NPMAX, wide, 0) & 15),
+                            1.0, 0.0)
+    fold_slot = iota(wide, FOLD, 1) - BMAX * group_of(wide, FOLD, 1, BMAX, K)
+    fold_from = iota(wide, FOLD, 0) - BMAX * group_of(wide, FOLD, 0, BMAX, NPMAX)
+    fold[...] = jnp.where((fold_slot == fold_from) & (iota(wide, FOLD, 1) < K * BMAX), 1.0, 0.0).astype(BF16)
+    own.wait()
+    loads[0].wait()
+    ahead = lax.dot_general(pan_ref[col, HALO:HALO + rows // 2, :], vec[early, :], (((0,), (0,)), ((), ())),
+                            preferred_element_type=F32)
     pl.semaphore_wait(barrier, len(greeted))
 
     def remote(src, dst, sems, slot, target):
@@ -90,11 +104,9 @@
             halos.append(remote(panel_hbm.at[pl.ds(src_at, HALO)], pan_ref.at[col, pl.ds(dst_at, HALO)],
                                 pan_sems, (1 + 2 * side + where,), (target, to)))
         halos.append(remote(vec_hbm.at[pl.ds(src_at, HALO)], halo_ref.at[side], halo_sems, (side,), (target, col)))
-    own.wait()
-    loads.wait()
-
-    def product(which, source):
-        piece = lax.dot_general(source, vec[...], (((0,), (0,)), ((), ())), preferred_element_type=F32)
+    loads[1].wait()
+
+    def product(which, piece):
         piece = piece.T.astype(BF16)
         for z in range(q):
             for at in range(p):
@@ -109,23 +121,19 @@
         return remote(middle.at[which, pl.ds(at, slab)], got_line.at[which, step], line_sems, (which, step),
                       (line_peer(step), col))
 
-    product(col, pan_ref[col, HALO:HALO + rows, :])
+    contract = (((0,), (0,)), ((), ()))
+    product(col, ahead + lax.dot_general(pan_ref[col, HALO + rows // 2:HALO + rows, :], vec[late, :], contract,
+                                         preferred_element_type=F32))
     for step in range(1, p):
         plane_copy(col, step).start()
     swap.wait_recv()
-    product(other, pan_ref[other, HALO:HALO + rows, :])
+    product(other, lax.dot_general(pan_ref[other, HALO:HALO + rows, :], vec[...], contract,
+                                   preferred_element_type=F32))
     for step in range(1, p):
         plane_copy(other, step).start()
     for copy in halos:
         copy.start()
 
-    atoms = cm_ref.shape[1]
-    wide = cm_ref.shape[2]
-    spread[...] = jnp.where(group_of(GROUP * NPMAX, wide, 1, BMAX, NPMAX) == (iota(GROUP * NPMAX, wide, 0) & 15),
-                            1.0, 0.0)
-    fold_slot = iota(wide, FOLD, 1) - BMAX * group_of(wide, FOLD, 1, BMAX, K)
-    fold_from = iota(wide, FOLD, 0) - BMAX * group_of(wide, FOLD, 0, BMAX, NPMAX)
-    fold[...] = jnp.where((fold_slot == fold_from) & (iota(wide, FOLD, 1) < K * BMAX), 1.0, 0.0).astype(BF16)
     for copy in count_copies:
         copy.wait_recv()
     blocks.wait()
@@ -366,7 +374,7 @@
             pltpu.VMEM((2, ext_rows + BMAX, half), F32),
             pltpu.VMEM((pad_rows, cols), BF16),
             pltpu.VMEM((pad_rows, npan), BF16),
-            dma, dma, dma, dma, dma((2, 5)), dma((2, 2)), dma((2, 2)),
+            dma((2,)), dma, dma, dma, dma((2, 5)), dma((2, 2)), dma((2, 2)),
             dma((2, 2, plane)), dma((2, 2, n // plane)), dma((2, n // plane)), dma((2, n // plane, plane)),
         ],
         compiler_params=pltpu.CompilerParams(collective_id=0, has_side_effects=True, vmem_limit_bytes=40 << 20),

time: 49.9 us -> 49.8 us (level)
  no operation moved by 1% of the time
where the time goes in v5:
time: 49.8 us; the launch traced here: 49.5 us
  Pallas kernels  46.9 us (94%)
  waiting for transfers between devices  1.24 us (2%)
  between operations  0.7 us (1%)
  other arithmetic  0.64 us (1%)
    pallas_call x1, Pallas kernels, local(): pl.pallas_call(functools.partial(mix_kernel, n, plane), out_shape=(jax.Sh...  37.2 us
    pallas_call x1, Pallas kernels, local(): pl.pallas_call(functools.partial(density_kernel, column_total=cols * lax....  9.67 us
    ppermute x1, waiting for transfers between devices, local(): lax.ppermute(sent, 'col', [(i, (i + step) % ncol) for i in range(ncol)])  1.24 us
  transfers between devices with their start and end apart: 1, of which 1 were waited for; matrix products, arithmetic and copies ran while one was open for 0% of the time, Pallas kernels for 0%

profile of v5, /device:TPU:0, one launch (start us, length us, event | category | flops | bytes accessed | tf_op | source)
XLA Modules:
  0.0 49.5 jit_solution(3367537360516977664)
XLA Ops:
  0.6 0.0 copy-start
  0.7 0.0 copy-start.1
  0.7 37.2 %shard_map.104 = (bf16[1024,256]{1,0:T(8,128)(2,1)S(1)}, bf16[2,2240,128]{2,1,0:T(8,128)(2,1)S(1)}, f32[8,256,1024]{2,1,0:T(8,128)S(1)}, bf16[8,256,256]{2,1,0:T(8,128)(2,1)S(1)}) custom-call(bf16[2048,1024]{1,0:T(8,128)(2,1)} %vin_ref.1, bf16[2048,128]{1,0:T(8,128)(2,1)} %panel_hbm.1, bf16[9,128,384]{2,1,0:T(8,128)(2,1)} %bitcast.7, f32[256,256]{1,0:T(8,128)} %factor_ref.1, ...), custom_call_target="tpu_custom_call" | custom-call | flops 8000000000 | bytes 10485760 | tf_op jit(solution)/shard_map/pallas_call | solution.py:348
  37.9 0.0 copy-done
  37.9 0.0 copy-done.1
  37.9 9.7 %shard_map.105 = (bf16[2048,1024]{1,0:T(8,128)(2,1)}, f32[128,256]{1,0:T(8,128)S(1)}) custom-call(bf16[2048,1024]{1,0:T(8,128)(2,1)} %vin_ref.1, bf16[2,2240,128]{2,1,0:T(8,128)(2,1)S(1)} %get-tuple-element.8.pan_ref, bf16[1024,256]{1,0:T(8,128)(2,1)S(1)} %get-tuple-element.9.mix_ref, f32[8,256,1024]{2,1,0:T(8,128)S(1)} %get-tuple-element.10.base_ref, ...), custom_call_target="tpu_custom_call" | custom-call | flops 6000000000 | bytes 10485760 | tf_op jit(solution)/shard_map/pallas_call | solution.py:385
  47.6 0.0 collective-permute-start
  47.6 1.2 %collective-permute-done = f32[64,256]{1,0:T(8,128)S(1)} collective-permute-done((f32[64,256]{1,0:T(8,128)S(1)}, f32[64,256]{1,0:T(8,128)S(1)}, u32[]{:S(2)}, u32[]{:S(2)}) %collective-permute-start) | collective-permute-done | bytes 65568 | tf_op jit(solution)/shard_map/ppermute | solution.py:408
  48.9 0.6 %dynamic-slice_add_fusion = f32[64,256]{1,0:T(8,128)} fusion(f32[64,256]{1,0:T(8,128)S(1)} %collective-permute-done, f32[128,256]{1,0:T(8,128)S(1)} %get-tuple-element.13, s32[]{:T(128)S(6)} %select_n.6), kind=kLoop, calls=%fused_computation | loop fusion | flops 16384 | bytes 196612 | tf_op jit(solution)/shard_map/add | solution.py:408
  (1 shorter events, 0.0 us)
Async XLA Ops:
  0.6 37.2 %copy-start = (s32[1024]{0:T(1024)S(1)}, s32[1024]{0:T(1024)}, u32[]{:S(2)}) copy-start(s32[1024]{0:T(1024)} %param.16) | copy-start | bytes 12292
  0.7 37.2 %copy-start.1 = (f32[1024]{0:T(1024)S(1)}, f32[1024]{0:T(1024)}, u32[]{:S(2)}) copy-start(f32[1024]{0:T(1024)} %param.17) | copy-start | bytes 12292
  47.6 1.3 %collective-permute-start = (f32[64,256]{1,0:T(8,128)S(1)}, f32[64,256]{1,0:T(8,128)S(1)}, u32[]{:S(2)}, u32[]{:S(2)}) collective-permute-start(f32[64,256]{1,0:T(8,128)S(1)} %constant_dynamic-slice_fusion), channel_id=1, source_target_pairs={{0,1},{1,0},{2,3},{3,2},{4,5},{5,4},{6,7},{7,6},{8,9},{9,8},{10,11... | collective-permute-start | bytes 196616 | tf_op jit(solution)/shard_map/ppermute | solution.py:408
